TPU v7x, 768 devices: a whole 4x8x12 slice. The times are simulated.
768 devices in a mesh: ctx: 96 (over x, z, core), dp: 8 (over y).
Axes of the slice: x: 4, y: 8, z: 12, core: 2. Of those that a mesh axis runs over, the one named last changes fastest.
Arguments:
- query: bfloat16 [8, 12288, 1024], P('dp', 'ctx')
- key: bfloat16 [8, 12288, 1024], P('dp', 'ctx')
- value: bfloat16 [8, 12288, 1024], P('dp', 'ctx'), may hold values from -5 to 5
- dout: bfloat16 [8, 12288, 1024], P('dp', 'ctx'), may hold values from -5 to 5
- glob_keys: bfloat16 [4, 64, 1024], replicated, may hold values from -5 to 5
- glob_values: bfloat16 [4, 64, 1024], replicated, may hold values from -5 to 5
- glob_ids: int32 [8, 2], P('dp'), may hold values from 0 to 3, all different within a row
- rand_blocks: int32 [8, 192, 3], replicated, may hold values from 0 to 191, as said below
Outputs:
- d_query: bfloat16 [8, 12288, 1024], P('dp', 'ctx')
- d_key: bfloat16 [8, 12288, 1024], P('dp', 'ctx')
- d_value: bfloat16 [8, 12288, 1024], P('dp', 'ctx')
- d_global: float32 [2, 4, 64, 1024], replicated
Inputs may be any that keep to these rules, and one draw needn't show every extreme that they name: With P = 96 and o_r = (r + 1) * P // 4, rand_blocks[h, i, r] lies in the span of blocks 2 * q to 2 * (q + 1) - 1, where q = (i // 2 + o_r) mod P.
All inputs are finite; a program needn't handle non-finite values.
Results may differ from a plain program's by a relative error of at most 0.015.
Values may be sent and summed in bfloat16 or wider, within the bound.
A program may use at most 64 MiB of HBM per device.

v0:
```python
import math

import jax
import jax.numpy as jnp
from jax import lax
from jax.sharding import PartitionSpec as P

BLK = 64


def passed_along(shard, axis, by):
    length = lax.axis_size(axis)
    return lax.ppermute(shard, axis, [(i, (i + by) % length) for i in range(length)])


def padded(cells, sides, width):
    for axis, dim in sides:
        count = lax.axis_size(axis)
        ends = count - 1
        head = lax.slice_in_dim(cells, 0, width, axis=dim)
        tail = lax.slice_in_dim(cells, cells.shape[dim] - width, cells.shape[dim], axis=dim)
        cells = jnp.concatenate(
            [
                lax.ppermute(tail, axis, [(i, (i + 1) % count) for i in range(ends)]),
                cells,
                lax.ppermute(head, axis, [((i + 1) % count, i) for i in range(ends)]),
            ],
            axis=dim,
        )
    return cells


def passed_along_2(value, axis, steps):
    count = lax.axis_size(axis)
    leading, last = (max(0, -steps), min(count, count - steps))
    return lax.ppermute(value, axis, [(source, source + steps) for source in range(leading, last)])


def attend(
    q_head,
    o_grad,
    k_head,
    v_head,
    gk_head,
    gv_head,
    key_index,
    key_valid,
    scatter_count,
    rand_count,
):
    q_blocks = q_head.shape[0]
    head_size = q_head.shape[2]
    scaling = 1.0 / math.sqrt(head_size)
    local_lists = key_index.shape[1]
    keys_all = jnp.concatenate(
        [
            jnp.take(k_head, key_index, axis=0),
            jnp.broadcast_to(gk_head[None], (q_blocks,) + gk_head.shape),
        ],
        axis=1,
    ).reshape(q_blocks, -1, head_size)
    values_all = jnp.concatenate(
        [
            jnp.take(v_head, key_index, axis=0),
            jnp.broadcast_to(gv_head[None], (q_blocks,) + gv_head.shape),
        ],
        axis=1,
    ).reshape(q_blocks, -1, head_size)
    keep_mask = jnp.repeat(
        jnp.concatenate([key_valid, jnp.ones((q_blocks, 2), dtype=bool)], axis=1), BLK, axis=1
    )
    scores = (
        jnp.einsum("nqd,nkd->nqk", q_head, keys_all, preferred_element_type=jnp.float32) * scaling
    )
    scores = jnp.where(keep_mask[:, None, :], scores, -1e30)
    row_max = jnp.max(scores, axis=-1, keepdims=True)
    exp_scores = jnp.exp(scores - row_max)
    weights = exp_scores / jnp.sum(exp_scores, axis=-1, keepdims=True)
    weights_b = weights.astype(jnp.bfloat16)
    attn_out = jnp.einsum("nqk,nkd->nqd", weights_b, values_all, preferred_element_type=jnp.float32)
    row_dot = jnp.sum(o_grad.astype(jnp.float32) * attn_out, axis=-1, keepdims=True)
    prob_grad = jnp.einsum("nqd,nkd->nqk", o_grad, values_all, preferred_element_type=jnp.float32)
    score_grad = (weights * (prob_grad - row_dot) * scaling).astype(jnp.bfloat16)
    q_grad = jnp.einsum("nqk,nkd->nqd", score_grad, keys_all, preferred_element_type=jnp.float32)
    k_grad = jnp.einsum(
        "nqk,nqd->nkd", score_grad, q_head, preferred_element_type=jnp.float32
    ).reshape(q_blocks, local_lists + 2, BLK, head_size)
    v_grad = jnp.einsum(
        "nqk,nqd->nkd", weights_b, o_grad, preferred_element_type=jnp.float32
    ).reshape(q_blocks, local_lists + 2, BLK, head_size)
    flat_index = key_index.reshape(-1)
    k_local = (
        jnp.zeros(k_head.shape, jnp.float32)
        .at[flat_index]
        .add(k_grad[:, :scatter_count].reshape(-1, BLK, head_size))
    )
    v_local = (
        jnp.zeros(v_head.shape, jnp.float32)
        .at[flat_index]
        .add(v_grad[:, :scatter_count].reshape(-1, BLK, head_size))
    )
    grad_tiles = score_grad.reshape(q_blocks, BLK, local_lists + 2, BLK)[
        :, :, 3 : 3 + rand_count
    ].transpose(0, 2, 1, 3)
    prob_tiles = weights_b.reshape(q_blocks, BLK, local_lists + 2, BLK)[
        :, :, 3 : 3 + rand_count
    ].transpose(0, 2, 1, 3)
    return (
        q_grad,
        k_local,
        v_local,
        k_grad[:, local_lists:],
        v_grad[:, local_lists:],
        grad_tiles,
        prob_tiles,
    )


def by_heads(row_array, head_count):
    block_total = row_array.shape[0] // BLK
    return row_array.reshape(block_total, BLK, head_count, -1).transpose(2, 0, 1, 3)


def from_heads(head_array):
    head_count = head_array.shape[0]
    head_size = head_array.shape[3]
    return head_array.transpose(1, 2, 0, 3).reshape(-1, head_count * head_size)


def fetch_far(key_value, offset):
    return passed_along(key_value, "ctx", -offset)


def return_far(partials, offset):
    return passed_along(partials, "ctx", offset)


def on_device(query, key, value, dout, glob_keys, glob_values, glob_ids, rand_blocks):
    row_count = query.shape[1]
    head_count = rand_blocks.shape[0]
    rand_count = rand_blocks.shape[2]
    head_size = query.shape[2] // head_count
    per_device = row_count // BLK
    span_count = lax.axis_size("ctx")
    device_pos = lax.axis_index("ctx")
    block_count = per_device * span_count
    offsets = [(slot + 1) * span_count // (rand_count + 1) for slot in range(rand_count)]
    key_value = jnp.stack([key[0], value[0]])
    extended = padded(key_value, (("ctx", 1),), row_count)
    far_spans = [fetch_far(key_value, offset) for offset in offsets]
    k_rows = jnp.concatenate([extended[0]] + [span[0] for span in far_spans], axis=0)
    v_rows = jnp.concatenate([extended[1]] + [span[1] for span in far_spans], axis=0)
    first_block = device_pos * per_device
    key_base = first_block - per_device
    query_ids = first_block + jnp.arange(per_device, dtype=jnp.int32)
    window = query_ids[:, None] + jnp.arange(-1, 2, dtype=jnp.int32)[None, :]
    key_valid = jnp.concatenate(
        [(window >= 0) & (window < block_count), jnp.ones((per_device, rand_count), dtype=bool)],
        axis=1,
    )
    window_local = jnp.clip(window - key_base, 0, 3 * per_device - 1)
    rand_rows = lax.dynamic_slice_in_dim(rand_blocks, first_block, per_device, 1)
    offset_table = jnp.array(offsets, dtype=jnp.int32)
    far_starts = (device_pos + offset_table) % span_count * per_device
    slot_base = (3 + jnp.arange(rand_count, dtype=jnp.int32)) * per_device
    rand_local = rand_rows - far_starts[None, None, :] + slot_base[None, None, :]
    all_lists = jnp.concatenate(
        [jnp.broadcast_to(window_local[None], (head_count,) + window_local.shape), rand_local],
        axis=2,
    )
    key_index = jnp.clip(all_lists, 0, (3 + rand_count) * per_device - 1)
    chosen = glob_ids[0]
    gk_heads = by_heads(jnp.take(glob_keys, chosen, axis=0).reshape(2 * BLK, -1), head_count)
    gv_heads = by_heads(jnp.take(glob_values, chosen, axis=0).reshape(2 * BLK, -1), head_count)
    scatter_count = 3 + rand_count

    def per_head(pieces):
        q_head, o_grad, k_head, v_head, gk_head, gv_head, index_head = pieces
        return attend(
            q_head,
            o_grad,
            k_head,
            v_head,
            gk_head,
            gv_head,
            index_head,
            key_valid,
            scatter_count,
            rand_count,
        )

    results = lax.map(
        per_head,
        (
            by_heads(query[0], head_count),
            by_heads(dout[0], head_count),
            by_heads(k_rows, head_count),
            by_heads(v_rows, head_count),
            gk_heads,
            gv_heads,
            key_index,
        ),
    )
    q_grad = results[0]
    kv_grads = jnp.stack([results[1], results[2]])
    lower_part = kv_grads[:, :, :per_device]
    upper_part = kv_grads[:, :, 2 * per_device : 3 * per_device]
    from_below = passed_along_2(upper_part.astype(jnp.bfloat16), "ctx", 1).astype(upper_part.dtype)
    from_above = passed_along_2(lower_part.astype(jnp.bfloat16), "ctx", -1).astype(lower_part.dtype)
    own_grads = kv_grads[:, :, per_device : 2 * per_device] + from_below + from_above
    for slot in range(rand_count):
        start = (3 + slot) * per_device
        own_grads = own_grads + return_far(
            kv_grads[:, :, start : start + per_device], offsets[slot]
        )
    global_part = jnp.stack([jnp.sum(results[3], axis=1), jnp.sum(results[4], axis=1)])
    global_part = global_part.transpose(0, 2, 3, 1, 4).reshape(2, 2, BLK, head_count * head_size)
    one_hot = (chosen[:, None] == jnp.arange(glob_keys.shape[0], dtype=jnp.int32)[None, :]).astype(
        jnp.float32
    )
    table_term = jnp.einsum("sg,ksbd->kgbd", one_hot, global_part, precision=lax.Precision.HIGHEST)
    table_grad = lax.psum(table_term, ("ctx", "dp"))
    d_query = from_heads(q_grad).astype(jnp.bfloat16)[None]
    d_key = from_heads(own_grads[0]).astype(jnp.bfloat16)[None]
    d_value = from_heads(own_grads[1]).astype(jnp.bfloat16)[None]
    return (d_query, d_key, d_value, table_grad)


def solution(mesh):
    placed = (
        P("dp", "ctx", None),
        P("dp", "ctx", None),
        P("dp", "ctx", None),
        P("dp", "ctx", None),
        P(),
        P(),
        P("dp", None),
        P(),
    )
    return jax.shard_map(
        on_device,
        mesh=mesh,
        in_specs=placed,
        out_specs=(P("dp", "ctx", None), P("dp", "ctx", None), P("dp", "ctx", None), P()),
        check_vma=False,
    )
```

profile of v0, /device:TPU:1, one launch (start us, length us, event | category | flops | bytes accessed | tf_op | source)
XLA Modules:
  0.0 691.5 jit_solution(15383519203984992578)
XLA Ops:
  9.3 4.0 collective-permute-start.4
  13.2 4.4 collective-permute-start.3
  17.6 3.1 collective-permute-start.2
  20.7 10.0 %collective-permute-start.1 = (bf16[2,128,1024]{2,1,0:T(8,128)(2,1)S(1)}, bf16[2,128,1024]{2,1,0:T(8,128)(2,1)}, u32[]{:S(2)}, u32[]{:S(2)}) collective-permute-start(bf16[2,128,1024]{2,1,0:T(8,128)(2,1)S(1)} %constant_dynamic-update-slice_fusion), channel_id=1, source_target_pairs={{8,0},{16,8},{24,16},{32,24},{40,32},{48,40},{56,48},{64,56},{72,6... | collective-permute-start | bytes 1572872 | tf_op jit(solution)/shard_map/ppermute | solution.py:26
  30.7 1.9 collective-permute-start
  36.1 1.6 gather_fusion.2
  40.5 1.3 pad_maximum_fusion.3
  44.1 3.7 maximum_bitcast_fusion
  48.4 1.6 copy.31
  50.5 1.6 copy.34
  52.1 113.2 %while.19 = (s32[]{:T(128)}, bf16[8,2,64,128]{3,2,1,0:T(8,128)(2,1)}, f32[8,12,64,128]{3,2,1,0:T(8,128)}, f32[8,12,64,128]{3,2,1,0:T(8,128)}, f32[8,2,2,64,128]{...) while((s32[]{:T(128)}, ...), condition=%wide.region_6.9_spmd.clone, body=%wide.region_0.8_spmd.clone.sunk | while | flops 102353728 | bytes 15382599 | solution.py:192
  104.3 1.3 scatter_fusion
  165.3 1.3 reduce_sum.37
  166.6 1.3 reduce_sum.36
  169.3 3.7 convolution_bitcast_fusion.1
  173.0 3.3 fusion.38
  176.3 2.5 collective-permute-start.7
  178.8 4.0 collective-permute-start.8
  182.8 4.1 collective-permute-start.9
  188.4 3.6 collective-permute-start.5
  192.0 8.1 %collective-permute-start.6 = (bf16[2,8,2,64,128]{4,3,2,1,0:T(8,128)(2,1)S(1)}, bf16[2,8,2,64,128]{4,3,2,1,0:T(8,128)(2,1)}, u32[]{:S(2)}, u32[]{:S(2)}) collective-permute-start(bf16[2,8,2,64,128]{4,3,2,1,0:T(8,128)(2,1)S(1)} %get-tuple-element.207), channel_id=1, source_target_pairs={{8,0},{16,8},{24,16},{32,24},{40,32},{48,40},{56,48},{64,56},{72,6... | collective-permute-start | bytes 1572872 | tf_op jit(solution)/shard_map/ppermute | solution.py:36
  202.0 473.4 %all-reduce.2.cloned.1.call-done = f32[2,4,64,1024]{3,1,2,0:T(4,128)} async-done(((f32[2,4,64,1024]{3,1,2,0:T(4,128)}), f32[2,4,64,1024]{3,1,2,0:T(4,128)}) %all-reduce.2.cloned.1.call-update) | async-done | bytes 2097168 | tf_op jit(solution)/shard_map/psum | solution.py:222
  675.4 4.3 copy.40
  679.7 2.9 fusion.41
  (398 shorter events, 128.8 us)
Async XLA Ops:
  7.2 28.4 %copy-start = (bf16[4,64,1024]{2,1,0:T(8,128)(2,1)S(1)}, bf16[4,64,1024]{2,1,0:T(8,128)(2,1)}, u32[]{:S(2)}) copy-start(bf16[4,64,1024]{2,1,0:T(8,128)(2,1)} %param.20) | copy-start | bytes 1572868
  7.2 30.9 %copy-start.4 = (bf16[1,128,1024]{2,1,0:T(8,128)(2,1)S(1)}, bf16[1,128,1024]{2,1,0:T(8,128)(2,1)}, u32[]{:S(2)}) copy-start(bf16[1,128,1024]{2,1,0:T(8,128)(2,1)} %param.15) | copy-start | bytes 786436
  7.2 30.9 %copy-start.5 = (bf16[1,128,1024]{2,1,0:T(8,128)(2,1)S(1)}, bf16[1,128,1024]{2,1,0:T(8,128)(2,1)}, u32[]{:S(2)}) copy-start(bf16[1,128,1024]{2,1,0:T(8,128)(2,1)} %param.18) | copy-start | bytes 786436
  7.2 668.2 %all-reduce.2.cloned.1.call-start = ((), (), s32[]{:S(2)}) async-start(), calls=%async_computation | async-start | bytes 4194304 | tf_op jit(solution)/shard_map/psum | solution.py:222
  9.3 32.5 %collective-permute-start.4 = (bf16[2,128,1024]{2,1,0:T(8,128)(2,1)S(1)}, bf16[2,128,1024]{2,1,0:T(8,128)(2,1)}, u32[]{:S(2)}, u32[]{:S(2)}) collective-permute-start(bf16[2,128,1024]{2,1,0:T(8,128)(2,1)S(1)} %constant_dynamic-update-slice_fusion), channel_id=1, source_target_pairs={{0,192},{8,200},{16,208},{24,216},{32,224},{40,232},{48,240},{56,2... | collective-permute-start | bytes 1572872 | tf_op jit(solution)/shard_map/ppermute | solution.py:13
  13.2 29.6 %collective-permute-start.3 = (bf16[2,128,1024]{2,1,0:T(8,128)(2,1)S(1)}, bf16[2,128,1024]{2,1,0:T(8,128)(2,1)}, u32[]{:S(2)}, u32[]{:S(2)}) collective-permute-start(bf16[2,128,1024]{2,1,0:T(8,128)(2,1)S(1)} %constant_dynamic-update-slice_fusion), channel_id=1, source_target_pairs={{0,384},{8,392},{16,400},{24,408},{32,416},{40,424},{48,432},{56,4... | collective-permute-start | bytes 1572872 | tf_op jit(solution)/shard_map/ppermute | solution.py:13
  17.6 26.5 %collective-permute-start.2 = (bf16[2,128,1024]{2,1,0:T(8,128)(2,1)S(1)}, bf16[2,128,1024]{2,1,0:T(8,128)(2,1)S(1)}, u32[]{:S(2)}, u32[]{:S(2)}) collective-permute-start(bf16[2,128,1024]{2,1,0:T(8,128)(2,1)S(1)} %constant_dynamic-update-slice_fusion), channel_id=1, source_target_pairs={{0,576},{8,584},{16,592},{24,600},{32,608},{40,616},{48,624},{56,6... | collective-permute-start | bytes 1572872 | tf_op jit(solution)/shard_map/ppermute | solution.py:13
  20.7 19.8 %collective-permute-start.1 = (bf16[2,128,1024]{2,1,0:T(8,128)(2,1)S(1)}, bf16[2,128,1024]{2,1,0:T(8,128)(2,1)}, u32[]{:S(2)}, u32[]{:S(2)}) collective-permute-start(bf16[2,128,1024]{2,1,0:T(8,128)(2,1)S(1)} %constant_dynamic-update-slice_fusion), channel_id=1, source_target_pairs={{8,0},{16,8},{24,16},{32,24},{40,32},{48,40},{56,48},{64,56},{72,6... | collective-permute-start | bytes 1572872 | tf_op jit(solution)/shard_map/ppermute | solution.py:26
  30.7 9.7 %collective-permute-start = (bf16[2,128,1024]{2,1,0:T(8,128)(2,1)S(1)}, bf16[2,128,1024]{2,1,0:T(8,128)(2,1)}, u32[]{:S(2)}, u32[]{:S(2)}) collective-permute-start(bf16[2,128,1024]{2,1,0:T(8,128)(2,1)S(1)} %constant_dynamic-update-slice_fusion), channel_id=1, source_target_pairs={{0,8},{8,16},{16,24},{24,32},{32,40},{40,48},{48,56},{56,64},{64,7... | collective-permute-start | bytes 1572872 | tf_op jit(solution)/shard_map/ppermute | solution.py:24
  168.0 1.3 copy-start.6
  173.0 13.9 %copy-start.1 = (f32[8,12,64,128]{3,2,1,0:T(8,128)S(1)}, f32[8,12,64,128]{3,2,1,0:T(8,128)}, u32[]{:S(2)}) copy-start(f32[8,12,64,128]{3,2,1,0:T(8,128)} %get-tuple-element.84) | copy-start | bytes 9437188
  173.0 13.9 %copy-start.3 = (f32[8,12,64,128]{3,2,1,0:T(8,128)S(1)}, f32[8,12,64,128]{3,2,1,0:T(8,128)}, u32[]{:S(2)}) copy-start(f32[8,12,64,128]{3,2,1,0:T(8,128)} %get-tuple-element.83) | copy-start | bytes 9437188
  176.3 503.4 %collective-permute-start.7 = (f32[2,8,2,64,128]{4,3,2,1,0:T(8,128)}, f32[2,8,2,64,128]{4,3,2,1,0:T(8,128)}, u32[]{:S(2)}, u32[]{:S(2)}) collective-permute-start(f32[2,8,2,64,128]{4,3,2,1,0:T(8,128)} %get-tuple-element.203), channel_id=1, source_target_pairs={{0,192},{8,200},{16,208},{24,216},{32,224},{40,232},{48,240},{56,2... | collective-permute-start | bytes 3145736 | tf_op jit(solution)/shard_map/ppermute | solution.py:13
  178.8 500.9 %collective-permute-start.8 = (f32[2,8,2,64,128]{4,3,2,1,0:T(8,128)S(1)}, f32[2,8,2,64,128]{4,3,2,1,0:T(8,128)}, u32[]{:S(2)}, u32[]{:S(2)}) collective-permute-start(f32[2,8,2,64,128]{4,3,2,1,0:T(8,128)S(1)} %get-tuple-element.204), channel_id=1, source_target_pairs={{0,384},{8,392},{16,400},{24,408},{32,416},{40,424},{48,432},{56,4... | collective-permute-start | bytes 3145736 | tf_op jit(solution)/shard_map/ppermute | solution.py:13
  182.8 496.9 %collective-permute-start.9 = (f32[2,8,2,64,128]{4,3,2,1,0:T(8,128)S(1)}, f32[2,8,2,64,128]{4,3,2,1,0:T(8,128)}, u32[]{:S(2)}, u32[]{:S(2)}) collective-permute-start(f32[2,8,2,64,128]{4,3,2,1,0:T(8,128)S(1)} %get-tuple-element.205), channel_id=1, source_target_pairs={{0,576},{8,584},{16,592},{24,600},{32,608},{40,616},{48,624},{56,6... | collective-permute-start | bytes 3145736 | tf_op jit(solution)/shard_map/ppermute | solution.py:13
  188.4 491.2 %collective-permute-start.5 = (bf16[2,8,2,64,128]{4,3,2,1,0:T(8,128)(2,1)}, bf16[2,8,2,64,128]{4,3,2,1,0:T(8,128)(2,1)}, u32[]{:S(2)}, u32[]{:S(2)}) collective-permute-start(bf16[2,8,2,64,128]{4,3,2,1,0:T(8,128)(2,1)} %get-tuple-element.206), channel_id=1, source_target_pairs={{0,8},{8,16},{16,24},{24,32},{32,40},{40,48},{48,56},{56,64},{64,7... | collective-permute-start | bytes 1572872 | tf_op jit(solution)/shard_map/ppermute | solution.py:36
  192.0 487.6 %collective-permute-start.6 = (bf16[2,8,2,64,128]{4,3,2,1,0:T(8,128)(2,1)S(1)}, bf16[2,8,2,64,128]{4,3,2,1,0:T(8,128)(2,1)}, u32[]{:S(2)}, u32[]{:S(2)}) collective-permute-start(bf16[2,8,2,64,128]{4,3,2,1,0:T(8,128)(2,1)S(1)} %get-tuple-element.207), channel_id=1, source_target_pairs={{8,0},{16,8},{24,16},{32,24},{40,32},{48,40},{56,48},{64,56},{72,6... | collective-permute-start | bytes 1572872 | tf_op jit(solution)/shard_map/ppermute | solution.py:36
  675.4 4.3 copy-start.2
Sparse Core Ops, SparseCore 0:
  173.1 502.2 all-reduce.1
where the time goes:
time: 695 us; the launch traced here: 691 us
  waiting for transfers between devices  473 us (68%)
  local copies, waits for them, and re-layouts  66.3 us (10%)
  other arithmetic  49.1 us (7%)
  starting transfers between devices  45.6 us (7%)
  matrix products  41.2 us (6%)
  between operations  14.5 us (2%)
    psum x1, waiting for transfers between devices, on_device(): table_grad = lax.psum(table_term, ('ctx', 'dp'))  473 us
    ppermute x6, starting transfers between devices, passed_along(): lax.ppermute(shard, axis, [(i, (i + by) % length) for i in range(length)])  22 us
    squeeze x16, local copies, waits for them, and re-layouts, on_device(): lax.map(per_head, (by_heads(query[0], head_count), by_heads(dout[0], head...  15.1 us
  transfers between devices with their start and end apart: 11, of which 1 were waited for; matrix products, arithmetic and copies ran while one was open for 3% of the time, Pallas kernels for 0%

commit v1 on v0

v1 whole, which is shorter than its diff:
```python
import functools
import math

import jax
import jax.numpy as jnp
from jax import lax
from jax.experimental import pallas as pl
from jax.experimental.pallas import tpu as pltpu
from jax.sharding import PartitionSpec as P

BLK = 64
HS = 128
NX = 4
SLOTS = 3
TABLE = 4
MESH = pl.DeviceIdType.MESH
BF16 = jnp.bfloat16
F32 = jnp.float32


def dot_nt(a, b):
    return lax.dot_general(a, b, (((1,), (1,)), ((), ())), preferred_element_type=F32)


def dot_nn(a, b):
    return lax.dot_general(a, b, (((1,), (0,)), ((), ())), preferred_element_type=F32)


def dot_tn(a, b):
    return lax.dot_general(a, b, (((0,), (0,)), ((), ())), preferred_element_type=F32)


def body(
    nz,
    ny,
    hx,
    ids_ref,
    rand_ref,
    q_in,
    k_in,
    v_in,
    o_in,
    gk_in,
    gv_in,
    dq_out,
    dk_out,
    dv_out,
    dg_out,
    kv,
    qd,
    edge,
    tab,
    gsel,
    pt,
    dst,
    dqs,
    dkv,
    dkvb,
    edge_s,
    edge_r,
    gp,
    gpb,
    g_core,
    y_send,
    y_recv,
    z_send,
    z_recv,
    y_all,
    in_loc,
    in_snd,
    in_rcv,
    tab_sem,
    e_snd,
    e_rcv,
    b_snd,
    b_rcv,
    dq_loc,
    dq_snd,
    dq_rcv,
    dkv_loc,
    dkv_snd,
    dkv_rcv,
    c_snd,
    c_rcv,
    yr_snd,
    yr_rcv,
    zr_snd,
    zr_rcv,
    zg_snd,
    zg_rcv,
    yg_snd,
    yg_rcv,
    xg_loc,
    xg_snd,
    xg_rcv,
    cg_snd,
    cg_rcv,
):
    ring = nz * 2
    ctx = lax.axis_index("ctx")
    y = lax.axis_index("dp")
    x = ctx // ring
    pos = ctx % ring
    z = pos // 2
    c = pos % 2
    wide = hx * HS
    scaling = 1.0 / math.sqrt(HS)
    own_cols = pl.multiple_of(x * wide, HS)
    up = x * ring + (pos + 1) % ring
    low = x * ring + (pos + ring - 1) % ring
    sib = x * ring + z * 2 + (1 - c)
    far = x * ring + jnp.where(c == 0, (pos + ring - 1) % ring, (pos + 1) % ring)

    def at_x(step):
        return (x + step) % NX

    def ctx_x(xs):
        return xs * ring + pos

    def ctx_z(zs):
        return x * ring + zs * 2 + c

    def remote(src, dst_ref, snd, rcv, to_ctx, to_y):
        return pltpu.make_async_remote_copy(
            src_ref=src,
            dst_ref=dst_ref,
            send_sem=snd,
            recv_sem=rcv,
            device_id={"ctx": to_ctx, "dp": to_y},
            device_id_type=MESH,
        )

    tab_copies = []
    for t, table in enumerate((gk_in, gv_in)):
        copy = pltpu.make_async_copy(table.at[:, :, pl.ds(own_cols, wide)], tab.at[t], tab_sem.at[t])
        copy.start()
        tab_copies.append(copy)

    tensors = (k_in, v_in, q_in, o_in)

    def land(h, t, xs):
        return (kv if t < 2 else qd).at[h, (t % 2) * NX + xs]

    local_in = {}
    for t in range(4):
        for h in range(hx):
            copy = pltpu.make_async_copy(
                tensors[t].at[:, :, pl.ds(pl.multiple_of(x * wide + h * HS, HS), HS)],
                land(h, t, x),
                in_loc.at[h, t],
            )
            copy.start()
            local_in[h, t] = copy

    barrier = pltpu.get_barrier_semaphore()
    partners = [(ctx_x(at_x(j)), y) for j in range(1, NX)]
    partners += [(sib, y), (far, y)]
    partners += [(ctx, (y + j) % ny) for j in range(1, ny)]
    partners += [(ctx_z((z + j) % nz), y) for j in range(1, nz)]
    for to_ctx, to_y in partners:
        pl.semaphore_signal(barrier, inc=1, device_id={"ctx": to_ctx, "dp": to_y}, device_id_type=MESH)
    pl.semaphore_wait(barrier, len(partners))

    sends = []

    def send_in(h, t, j):
        to = at_x(j)
        copy = remote(
            tensors[t].at[:, :, pl.ds(pl.multiple_of(to * wide + h * HS, HS), HS)],
            land(h, t, x),
            in_snd.at[h, t, j - 1],
            in_rcv.at[h, t, j - 1],
            ctx_x(to),
            y,
        )
        copy.start()
        sends.append(copy)

    def wait_in(h, t):
        local_in[h, t].wait()
        for j in (1, 3, 2):
            frm = at_x(NX - j)
            remote(
                land(h, t, frm), land(h, t, frm), in_snd.at[h, t, j - 1], in_rcv.at[h, t, j - 1], ctx_x(frm), y
            ).wait_recv()

    for pair in ((0, 1), (2, 3)):
        for h in range(hx):
            for t in pair:
                for j in (2, 1, 3):
                    send_in(h, t, j)

    for copy in tab_copies:
        copy.wait()
    for h in range(hx):
        for t in range(2):
            for s in range(2):
                gsel[h, t, s] = tab[t, ids_ref[0, s], :, h * HS : (h + 1) * HS]

    edge_copies = {}
    for h in range(hx):
        wait_in(h, 0)
        wait_in(h, 1)
        for way, to in ((0, up), (1, low)):
            copy = remote(
                kv.at[h, :, 1 - way], edge.at[h, way], e_snd.at[h, way], e_rcv.at[h, way], to, y
            )
            copy.start()
            edge_copies[h, way] = copy
            sends.append(copy)

    seam_low = jnp.where(pos == 0, 1, 0)
    seam_up = jnp.where(pos == ring - 1, 1, 0)

    def compute(h):
        k_main = kv[h, 0:NX].reshape(NX * 2 * BLK, HS)
        v_main = kv[h, NX : 2 * NX].reshape(NX * 2 * BLK, HS)
        k_tab = gsel[h, 0].reshape(2 * BLK, HS)
        v_tab = gsel[h, 1].reshape(2 * BLK, HS)
        lane = lax.broadcasted_iota(jnp.int32, (1, 2 * BLK), 1)
        half = lane // BLK

        def span(xq, carry):
            q = qd[h, xq].reshape(2 * BLK, HS)
            g = qd[h, NX + xq].reshape(2 * BLK, HS)
            i_low = (xq + NX - seam_low) % NX
            i_up = (xq + seam_up) % NX
            k_edge = jnp.concatenate([edge[h, 0, i_low], edge[h, 1, i_up]], axis=0)
            v_edge = jnp.concatenate([edge[h, 0, NX + i_low], edge[h, 1, NX + i_up]], axis=0)
            s_main = dot_nt(k_main, q) * scaling
            s_tab = dot_nt(k_tab, q) * scaling
            s_edge = dot_nt(k_edge, q) * scaling
            block = 2 * (xq * ring + pos)
            pieces = []
            for xs in range(NX):
                slot = (xs + NX - xq - 1) % NX
                row = jnp.minimum(slot, SLOTS - 1)
                first = rand_ref[row, x * hx + h, block] % 2
                second = rand_ref[row, x * hx + h, block + 1] % 2
                own = jnp.where(slot == SLOTS, 1, 0)
                inside = jnp.where(half == 0, first, second)
                for b in range(2):
                    hit = jnp.where(inside == b, 1, own)
                    keep = jnp.broadcast_to(hit, (BLK, 2 * BLK)) > 0
                    at = (xs * 2 + b) * BLK
                    pieces.append(jnp.where(keep, s_main[at : at + BLK], -1e30))
            pieces += [s_tab[:BLK], s_tab[BLK:]]
            ok_low = jnp.where(jnp.logical_and(xq == 0, pos == 0), 0, 1)
            ok_up = jnp.where(jnp.logical_and(xq == NX - 1, pos == ring - 1), 0, 1)
            for b, ok in ((0, ok_low), (1, ok_up)):
                hit = jnp.where(half == b, ok, 0)
                keep = jnp.broadcast_to(hit, (BLK, 2 * BLK)) > 0
                pieces.append(jnp.where(keep, s_edge[b * BLK : (b + 1) * BLK], -1e30))
            top = functools.reduce(jnp.maximum, pieces)
            top = jnp.max(top, axis=0, keepdims=True)
            exps = [jnp.exp(piece - top) for piece in pieces]
            total = jnp.sum(functools.reduce(jnp.add, exps), axis=0, keepdims=True)
            inverse = 1.0 / total
            d_main = dot_nt(v_main, g)
            d_tab = dot_nt(v_tab, g)
            d_edge = dot_nt(v_edge, g)
            d_pieces = [d_main[i * BLK : (i + 1) * BLK] for i in range(2 * NX)]
            d_pieces += [d_tab[:BLK], d_tab[BLK:], d_edge[:BLK], d_edge[BLK:]]
            probs = [e * inverse for e in exps]
            probs_b = [p.astype(BF16) for p in probs]
            dots = functools.reduce(
                jnp.add, [p.astype(F32) * d for p, d in zip(probs_b, d_pieces)]
            )
            row_dot = jnp.sum(dots, axis=0, keepdims=True)
            grads = [
                (p * (d - row_dot) * scaling).astype(BF16) for p, d in zip(probs, d_pieces)
            ]
            p_list = jnp.concatenate(probs_b[:10], axis=0)
            g_list = jnp.concatenate(grads[:10], axis=0)
            cols = pl.ds(pl.multiple_of(xq * 2 * BLK, 2 * BLK), 2 * BLK)
            pt[:, cols] = p_list
            dst[:, cols] = g_list
            g_edge = jnp.concatenate(grads[10:], axis=0)
            p_edge = jnp.concatenate(probs_b[10:], axis=0)
            dq = dot_tn(g_list[: NX * 2 * BLK], k_main)
            dq += dot_tn(g_list[NX * 2 * BLK :], k_tab)
            dq += dot_tn(g_edge, k_edge)
            dqs[h, xq] = dq.astype(BF16).reshape(2, BLK, HS)
            dk_edge = dot_nn(g_edge, q).astype(BF16)
            dv_edge = dot_nn(p_edge, g).astype(BF16)
            edge_s[h, 0, i_low] = dk_edge[:BLK]
            edge_s[h, 1, i_up] = dk_edge[BLK:]
            edge_s[h, 0, NX + i_low] = dv_edge[:BLK]
            edge_s[h, 1, NX + i_up] = dv_edge[BLK:]
            return carry

        lax.fori_loop(0, NX, span, 0)
        for t, lists in ((0, dst), (1, pt)):
            rows = qd[h, t * NX : (t + 1) * NX].reshape(NX * 2 * BLK, HS)
            grad = dot_nn(lists[...], rows)
            dkv[h, t * NX : (t + 1) * NX] = grad[: NX * 2 * BLK].reshape(NX, 2, BLK, HS)
            gp[t, :, :, h * HS : (h + 1) * HS] = grad[NX * 2 * BLK :].reshape(2, BLK, HS)

    back_copies = {}
    pending = []
    locals_out = []

    def out_cols(xs, h):
        return pl.ds(pl.multiple_of(xs * wide + h * HS, HS), HS)

    def send_out(out, src_of, h, snd, rcv, loc):
        for j in (2, 1, 3):
            to = at_x(j)
            copy = remote(
                src_of(to), out.at[:, :, out_cols(x, h)], snd(j - 1), rcv(j - 1), ctx_x(to), y
            )
            copy.start()
            sends.append(copy)
            frm = at_x(NX - j)
            pending.append(
                remote(
                    src_of(to), out.at[:, :, out_cols(frm, h)], snd(j - 1), rcv(j - 1), ctx_x(to), y
                )
            )
        copy = pltpu.make_async_copy(src_of(x), out.at[:, :, out_cols(x, h)], loc)
        copy.start()
        locals_out.append(copy)

    def after(h):
        for way, to in ((0, low), (1, up)):
            copy = remote(
                edge_s.at[h, way], edge_r.at[h, way], b_snd.at[h, way], b_rcv.at[h, way], to, y
            )
            copy.start()
            back_copies[h, way] = copy
            sends.append(copy)
        send_out(
            dq_out,
            lambda xs: dqs.at[h, xs],
            h,
            lambda j: dq_snd.at[h, j],
            lambda j: dq_rcv.at[h, j],
            dq_loc.at[h],
        )

    def finish(h):
        for way in range(2):
            back_copies[h, way].wait_recv()
        for t in range(2):
            for b in range(2):
                part = slice(t * NX, (t + 1) * NX)
                total = dkv[h, part, b] + edge_r[h, 1 - b, part].astype(F32)
                dkvb[h, part, b] = total.astype(BF16)
        for t, out in ((0, dk_out), (1, dv_out)):
            send_out(
                out,
                lambda xs, t=t: dkvb.at[h, t * NX + xs],
                h,
                lambda j, t=t: dkv_snd.at[h, t, j],
                lambda j, t=t: dkv_rcv.at[h, t, j],
                dkv_loc.at[h, t],
            )

    for h in range(hx):
        wait_in(h, 2)
        wait_in(h, 3)
        for way in range(2):
            edge_copies[h, way].wait_recv()
        compute(h)
        after(h)

    gpb[...] = gp[...].astype(BF16)
    core_copy = remote(gpb.at[1 - c], g_core, c_snd.at[0], c_rcv.at[0], sib, y)
    core_copy.start()
    sends.append(core_copy)
    for h in range(hx - 1):
        finish(h)
    core_copy.wait_recv()
    rows_y = TABLE * BLK // ny
    both = [gp[c, s] + g_core[s].astype(F32) for s in range(2)]
    per_block = BLK // rows_y
    for b in range(TABLE):
        value = jnp.where(ids_ref[0, 0] == b, both[0], 0.0) + jnp.where(ids_ref[0, 1] == b, both[1], 0.0)
        for r in range(per_block):
            y_send[b * per_block + r] = value[r * rows_y : (r + 1) * rows_y].astype(BF16)
    for j in range(1, ny):
        copy = remote(
            y_send.at[(y + j) % ny], y_recv.at[j - 1], yr_snd.at[j - 1], yr_rcv.at[j - 1], ctx, (y + j) % ny
        )
        copy.start()
        sends.append(copy)
    finish(hx - 1)
    for j in range(1, ny):
        remote(y_send.at[y], y_recv.at[j - 1], yr_snd.at[j - 1], yr_rcv.at[j - 1], ctx, y).wait_recv()
    total = y_send[y].astype(F32)
    for j in range(1, ny):
        total += y_recv[j - 1].astype(F32)
    parts = z_send.shape[0]
    rows_z = z_send.shape[1]
    every = nz // parts
    for k in range(parts):
        z_send[k] = total[k * rows_z : (k + 1) * rows_z].astype(BF16)
    is_owner = z % every == 0
    mine = z // every

    def z_reduce(k, j):
        return remote(
            z_send.at[k], z_recv.at[j - 1], zr_snd.at[j - 1], zr_rcv.at[j - 1], ctx_z((z + j) % nz), y
        )

    def z_gather(j, k):
        return remote(
            y_all.at[y, k], y_all.at[y, k], zg_snd.at[j - 1], zg_rcv.at[k], ctx_z((z + j) % nz), y
        )

    for j in range(1, nz):
        to = (z + j) % nz

        @pl.when(to % every == 0)
        def _(j=j, to=to):
            z_reduce(to // every, j).start()

    @pl.when(is_owner)
    def _():
        for j in range(1, nz):
            z_reduce(0, j).wait_recv()
        acc = z_send[mine].astype(F32)
        for j in range(1, nz):
            acc += z_recv[j - 1].astype(F32)
        y_all[y, mine] = acc.astype(BF16)
        for j in range(1, nz):
            z_gather(j, mine).start()

    for k in range(parts):

        @pl.when(z != k * every)
        def _(k=k):
            z_gather(1, k).wait_recv()

    for j in range(1, ny):
        copy = remote(
            y_all.at[y], y_all.at[y], yg_snd.at[j - 1], yg_rcv.at[j - 1], ctx, (y + j) % ny
        )
        copy.start()
        sends.append(copy)
    for j in range(1, ny):
        frm = (y + ny - j) % ny
        remote(y_all.at[frm], y_all.at[frm], yg_snd.at[j - 1], yg_rcv.at[j - 1], ctx, y).wait_recv()

    def table_out(xs, kind):
        return dg_out.at[kind, :, :, :, pl.ds(pl.multiple_of(xs * wide, HS), wide)]

    for j in (2, 1, 3):
        copy = remote(
            y_all, table_out(x, c), xg_snd.at[j - 1], xg_rcv.at[j - 1], ctx_x(at_x(j)), y
        )
        copy.start()
        sends.append(copy)
    copy = pltpu.make_async_copy(y_all, table_out(x, c), xg_loc.at[0])
    copy.start()
    locals_out.append(copy)

    def to_sibling(src, xs, j):
        copy = remote(src, table_out(xs, c), cg_snd.at[j], cg_rcv.at[j], sib, y)
        copy.start()
        sends.append(copy)
        pending.append(remote(src, table_out(xs, 1 - c), cg_snd.at[j], cg_rcv.at[j], sib, y))

    to_sibling(y_all, x, 0)
    for j in (1, 3, 2):
        frm = at_x(NX - j)
        remote(y_all, table_out(frm, c), xg_snd.at[j - 1], xg_rcv.at[j - 1], ctx_x(frm), y).wait_recv()
        to_sibling(table_out(frm, c), frm, j)

    for copy in pending:
        copy.wait_recv()
    for copy in locals_out:
        copy.wait()
    for copy in sends:
        copy.wait_send()
    for j in range(1, nz):
        to = (z + j) % nz

        @pl.when(to % every == 0)
        def _(j=j):
            z_reduce(0, j).wait_send()

        @pl.when(is_owner)
        def _(j=j):
            z_gather(j, mine).wait_send()


def on_device(nz, ny, query, key, value, dout, glob_keys, glob_values, glob_ids, rand_blocks):
    heads = rand_blocks.shape[0]
    hx = heads // NX
    hd = query.shape[2]
    wide = hx * HS
    rows_y = TABLE * BLK // ny
    parts = 4
    rows_z = rows_y // parts
    blocks = [a.reshape(2, BLK, hd) for a in (query, key, value, dout)]
    rand = jnp.transpose(rand_blocks, (2, 0, 1))
    vm = pltpu.VMEM
    dma = pltpu.SemaphoreType.DMA
    out = jax.ShapeDtypeStruct((2, BLK, hd), BF16)
    anywhere = pl.BlockSpec(memory_space=pl.ANY)
    scalars = pl.BlockSpec(memory_space=pltpu.SMEM)
    scratch = [
        vm((hx, 2 * NX, 2, BLK, HS), BF16),
        vm((hx, 2 * NX, 2, BLK, HS), BF16),
        vm((hx, 2, 2 * NX, BLK, HS), BF16),
        vm((2, TABLE, BLK, wide), BF16),
        vm((hx, 2, 2, BLK, HS), BF16),
        vm((10 * BLK, NX * 2 * BLK), BF16),
        vm((10 * BLK, NX * 2 * BLK), BF16),
        vm((hx, NX, 2, BLK, HS), BF16),
        vm((hx, 2 * NX, 2, BLK, HS), F32),
        vm((hx, 2 * NX, 2, BLK, HS), BF16),
        vm((hx, 2, 2 * NX, BLK, HS), BF16),
        vm((hx, 2, 2 * NX, BLK, HS), BF16),
        vm((2, 2, BLK, wide), F32),
        vm((2, 2, BLK, wide), BF16),
        vm((2, BLK, wide), BF16),
        vm((ny, rows_y, wide), BF16),
        vm((max(ny - 1, 1), rows_y, wide), BF16),
        vm((parts, rows_z, wide), BF16),
        vm((max(nz - 1, 1), rows_z, wide), BF16),
        vm((ny, parts, rows_z, wide), BF16),
        dma((hx, 4)),
        dma((hx, 4, 3)),
        dma((hx, 4, 3)),
        dma((2,)),
        dma((hx, 2)),
        dma((hx, 2)),
        dma((hx, 2)),
        dma((hx, 2)),
        dma((hx,)),
        dma((hx, 3)),
        dma((hx, 3)),
        dma((hx, 2)),
        dma((hx, 2, 3)),
        dma((hx, 2, 3)),
        dma((1,)),
        dma((1,)),
        dma((ny,)),
        dma((ny,)),
        dma((nz,)),
        dma((nz,)),
        dma((nz,)),
        dma((parts,)),
        dma((ny,)),
        dma((ny,)),
        dma((1,)),
        dma((3,)),
        dma((3,)),
        dma((4,)),
        dma((4,)),
    ]
    dq, dk, dv, dg = pl.pallas_call(
        functools.partial(body, nz, ny, hx),
        out_shape=(out, out, out, jax.ShapeDtypeStruct((2, ny, parts, rows_z, hd), BF16)),
        in_specs=[scalars, scalars] + [anywhere] * 6,
        out_specs=(anywhere,) * 4,
        scratch_shapes=scratch,
        compiler_params=pltpu.CompilerParams(
            collective_id=0, has_side_effects=True, vmem_limit_bytes=48 * 1024 * 1024
        ),
    )(glob_ids, rand, *blocks, glob_keys, glob_values)
    dq, dk, dv = (a.reshape(1, 2 * BLK, hd) for a in (dq, dk, dv))
    return dq, dk, dv, dg.reshape(2, TABLE, BLK, hd).astype(F32)


def solution(mesh):
    ny = mesh.shape["dp"]
    nz = mesh.shape["ctx"] // (2 * NX)
    split = P("dp", "ctx", None)
    return jax.shard_map(
        functools.partial(on_device, nz, ny),
        mesh=mesh,
        in_specs=(split, split, split, split, P(), P(), P("dp", None), P()),
        out_specs=(split, split, split, P()),
        check_vma=False,
    )
```

time: 695 us -> 84.5 us (0.12)
  waiting for transfers between devices: 473 us -> 0 us
  Pallas kernels: 0 us -> 72.5 us
  local copies, waits for them, and re-layouts: 66.3 us -> 9.37 us
  other arithmetic: 49.1 us -> 1.57 us
  starting transfers between devices: 45.6 us -> 0 us
  matrix products: 41.2 us -> 0 us
  between operations: 14.5 us -> 0.66 us
    psum x1 -> x0, waiting for transfers between devices: 473 us -> none  [on_device(): table_grad = lax.psum(table_term, ('ctx', 'dp'))]
    pallas_call x0 -> x1, Pallas kernels: none -> 72.5 us  [on_device(): pl.pallas_call(functools.partial(body, nz, ny, hx), out_shape=(out, out,...]
    ppermute x10 -> x0, starting transfers between devices: 45.6 us -> none  [the longest x6 22 us: passed_along(): lax.ppermute(shard, axis, [(i, (i + by) % length) for i in range(length)])]
    dot_general x49 -> x0, matrix products: 41.2 us -> none  [the longest x8 9.79 us: attend(): jnp.einsum('nqk,nkd->nqd', weights_b, values_all, preferred_element_type=...]
    scatter-add x16 -> x0, other arithmetic: 21.2 us -> none  [the longest x8 10.6 us: attend(): v_local = jnp.zeros(v_head.shape, jnp.float32).at[flat_index].add(v_grad[...]
    squeeze x20 -> x0, local copies, waits for them, and re-layouts: 17.4 us -> none  [the longest x16 15.1 us: on_device(): lax.map(per_head, (by_heads(query[0], head_count), by_heads(dout[0], head...]
    dynamic_update_slice x16 -> x0, local copies, waits for them, and re-layouts: 13.6 us -> none  [on_device(): lax.map(per_head, (by_heads(query[0], head_count), by_heads(dout[0], head...]
    gather x18 -> x0, local copies, waits for them, and re-layouts: 11.5 us -> none  [the longest x8 4.67 us: attend(): jnp.take(k_head, key_index, axis=0)]
  transfers between devices with their start and end apart: 11 -> 0, of which waited for: 1 -> 0; matrix products, arithmetic and copies ran while one was open for 3% -> 0% of each run, Pallas kernels for 0% -> 0%
where the time goes in v1:
time: 84.5 us; the launch traced here: 84.1 us
  Pallas kernels  72.5 us (86%)
  local copies, waits for them, and re-layouts  9.37 us (11%)
  other arithmetic  1.57 us (2%)
    pallas_call x1, Pallas kernels, on_device(): pl.pallas_call(functools.partial(body, nz, ny, hx), out_shape=(out, out,...  72.5 us
    unnamed x19, local copies, waits for them, and re-layouts  9.37 us

profile of v1, /device:TPU:1, one launch (start us, length us, event | category | flops | bytes accessed | tf_op | source)
XLA Modules:
  0.0 84.1 jit_solution(4803610141854148505)
XLA Ops:
  0.6 0.0 copy-start
  0.6 1.0 %copy-done = bf16[4,64,1024]{2,1,0:T(8,128)(2,1)S(1)} copy-done((bf16[4,64,1024]{2,1,0:T(8,128)(2,1)S(1)}, bf16[4,64,1024]{2,1,0:T(8,128)(2,1)}, u32[]{:S(2)}) %copy-start) | copy-done | bytes 524312
  1.7 0.0 copy-start.1
  1.7 1.0 %copy-done.1 = bf16[4,64,1024]{2,1,0:T(8,128)(2,1)S(1)} copy-done((bf16[4,64,1024]{2,1,0:T(8,128)(2,1)S(1)}, bf16[4,64,1024]{2,1,0:T(8,128)(2,1)}, u32[]{:S(2)}) %copy-start.1) | copy-done | bytes 524312
  2.7 0.0 copy-start.2
  2.7 0.9 %copy-done.2 = bf16[1,128,1024]{2,1,0:T(8,128)(2,1)S(1)} copy-done((bf16[1,128,1024]{2,1,0:T(8,128)(2,1)S(1)}, bf16[1,128,1024]{2,1,0:T(8,128)(2,1)}, u32[]{:S(2)}) %copy-start.2) | copy-done | bytes 262168
  3.7 0.0 copy-start.3
  3.7 0.9 %copy-done.3 = bf16[1,128,1024]{2,1,0:T(8,128)(2,1)S(1)} copy-done((bf16[1,128,1024]{2,1,0:T(8,128)(2,1)S(1)}, bf16[1,128,1024]{2,1,0:T(8,128)(2,1)}, u32[]{:S(2)}) %copy-start.3) | copy-done | bytes 262168
  4.6 0.0 copy-start.4
  4.6 0.9 %copy-done.4 = bf16[1,128,1024]{2,1,0:T(8,128)(2,1)S(1)} copy-done((bf16[1,128,1024]{2,1,0:T(8,128)(2,1)S(1)}, bf16[1,128,1024]{2,1,0:T(8,128)(2,1)}, u32[]{:S(2)}) %copy-start.4) | copy-done | bytes 262168
  5.6 0.0 copy-start.5
  5.6 0.9 %copy-done.5 = bf16[1,128,1024]{2,1,0:T(8,128)(2,1)S(1)} copy-done((bf16[1,128,1024]{2,1,0:T(8,128)(2,1)S(1)}, bf16[1,128,1024]{2,1,0:T(8,128)(2,1)}, u32[]{:S(2)}) %copy-start.5) | copy-done | bytes 262168
  6.5 0.0 copy-start.6
  6.5 0.7 copy-done.6
  7.3 0.0 copy-start.7
  7.3 0.7 copy-done.7
  7.9 72.5 %shard_map.111 = (bf16[2,64,1024]{2,1,0:T(8,128)(2,1)S(1)}, bf16[2,64,1024]{2,1,0:T(8,128)(2,1)S(1)}, bf16[2,64,1024]{2,1,0:T(8,128)(2,1)S(1)}, bf16[2,8,4,8,1024]{4,3,2,1,0:T(8,128)(2,1)S(1)}) custom-call(s32[1,2]{1,0:T(1,128)S(1)} %copy-done.7, s32[3,8,192]{2,1,0:T(8,128)S(1)} %bitcast.18, bf16[2,64,1024]{2,1,0:T(8,128)(2,1)S(1)} %bitcast.11, ...), custom_call_target="tpu_custom_call" | custom-call | tf_op jit(solution)/shard_map/pallas_call | solution.py:554
  80.4 1.6 %convert.1 = f32[2,4,64,1024]{3,2,1,0:T(8,128)} convert(bf16[2,4,64,1024]{3,2,1,0:T(8,128)(2,1)S(1)} %bitcast.10) | non-fusion elementwise | flops 524288 | bytes 3145728 | tf_op jit(solution)/shard_map/convert_element_type | solution.py:565
  81.9 0.7 copy.15
  82.7 0.7 copy.16
  83.4 0.7 copy.17
Async XLA Ops:
  0.6 1.0 %copy-start = (bf16[4,64,1024]{2,1,0:T(8,128)(2,1)S(1)}, bf16[4,64,1024]{2,1,0:T(8,128)(2,1)}, u32[]{:S(2)}) copy-start(bf16[4,64,1024]{2,1,0:T(8,128)(2,1)} %gk_in.1) | copy-start | bytes 1572868
  1.7 1.0 %copy-start.1 = (bf16[4,64,1024]{2,1,0:T(8,128)(2,1)S(1)}, bf16[4,64,1024]{2,1,0:T(8,128)(2,1)}, u32[]{:S(2)}) copy-start(bf16[4,64,1024]{2,1,0:T(8,128)(2,1)} %gv_in.1) | copy-start | bytes 1572868
  2.7 0.9 %copy-start.2 = (bf16[1,128,1024]{2,1,0:T(8,128)(2,1)S(1)}, bf16[1,128,1024]{2,1,0:T(8,128)(2,1)}, u32[]{:S(2)}) copy-start(bf16[1,128,1024]{2,1,0:T(8,128)(2,1)} %param.8) | copy-start | bytes 786436
  3.7 0.9 %copy-start.3 = (bf16[1,128,1024]{2,1,0:T(8,128)(2,1)S(1)}, bf16[1,128,1024]{2,1,0:T(8,128)(2,1)}, u32[]{:S(2)}) copy-start(bf16[1,128,1024]{2,1,0:T(8,128)(2,1)} %param.9) | copy-start | bytes 786436
  4.6 0.9 %copy-start.4 = (bf16[1,128,1024]{2,1,0:T(8,128)(2,1)S(1)}, bf16[1,128,1024]{2,1,0:T(8,128)(2,1)}, u32[]{:S(2)}) copy-start(bf16[1,128,1024]{2,1,0:T(8,128)(2,1)} %param.10) | copy-start | bytes 786436
  5.6 0.9 %copy-start.5 = (bf16[1,128,1024]{2,1,0:T(8,128)(2,1)S(1)}, bf16[1,128,1024]{2,1,0:T(8,128)(2,1)}, u32[]{:S(2)}) copy-start(bf16[1,128,1024]{2,1,0:T(8,128)(2,1)} %param.11) | copy-start | bytes 786436
  6.5 0.7 copy-start.6
  7.3 0.7 copy-start.7

commit v2 on v1

--- a/solution.py
+++ b/solution.py
@@ -28,6 +28,10 @@
 
 def dot_tn(a, b):
     return lax.dot_general(a, b, (((0,), (0,)), ((), ())), preferred_element_type=F32)
+
+
+def outward(count):
+    return sorted(range(1, count), key=lambda j: (-min(j, count - j), j))
 
 
 def body(
@@ -61,10 +65,10 @@
     gp,
     gpb,
     g_core,
+    ids_all,
     y_send,
     y_recv,
-    z_send,
-    z_recv,
+    z_all,
     y_all,
     in_loc,
     in_snd,
@@ -82,12 +86,12 @@
     dkv_rcv,
     c_snd,
     c_rcv,
+    id_snd,
+    id_rcv,
     yr_snd,
     yr_rcv,
-    zr_snd,
-    zr_rcv,
-    zg_snd,
-    zg_rcv,
+    z_snd,
+    z_rcv,
     yg_snd,
     yg_rcv,
     xg_loc,
@@ -189,6 +193,18 @@
             for t in pair:
                 for j in (2, 1, 3):
                     send_in(h, t, j)
+
+    for s in range(2):
+        ids_all[y, s] = jnp.full((BLK // ny, HS), ids_ref[0, s], jnp.int32)
+    id_waits = []
+    for j in range(1, ny):
+        to, frm = (y + j) % ny, (y + ny - j) % ny
+        copy = remote(ids_all.at[y], ids_all.at[y], id_snd.at[j - 1], id_rcv.at[j - 1], ctx, to)
+        copy.start()
+        sends.append(copy)
+        id_waits.append(
+            remote(ids_all.at[frm], ids_all.at[frm], id_snd.at[j - 1], id_rcv.at[j - 1], ctx, frm)
+        )
 
     for copy in tab_copies:
         copy.wait()
@@ -371,101 +387,109 @@
     for h in range(hx - 1):
         finish(h)
     core_copy.wait_recv()
-    rows_y = TABLE * BLK // ny
-    both = [gp[c, s] + g_core[s].astype(F32) for s in range(2)]
-    per_block = BLK // rows_y
+    rows_y = BLK // ny
+    for s in range(2):
+        both = (gp[c, s] + g_core[s].astype(F32)).astype(BF16)
+        for r in range(ny):
+            y_send[r, s] = both[r * rows_y : (r + 1) * rows_y]
+    for j in outward(ny):
+        to = (y + j) % ny
+        copy = remote(y_send.at[to], y_recv.at[y], yr_snd.at[j - 1], yr_rcv.at[j - 1], ctx, to)
+        copy.start()
+        sends.append(copy)
+    y_recv[y] = y_send[y]
+    finish(hx - 1)
+    for copy in id_waits:
+        copy.wait_recv()
+    for j in outward(ny)[::-1]:
+        frm = (y + ny - j) % ny
+        remote(y_send.at[y], y_recv.at[frm], yr_snd.at[j - 1], yr_rcv.at[j - 1], ctx, frm).wait_recv()
+    sums = [jnp.zeros((rows_y, wide), F32) for _ in range(TABLE)]
+    for src in range(ny):
+        for s in range(2):
+            chosen = jnp.concatenate([ids_all[src, s]] * hx, axis=1)
+            term = y_recv[src, s].astype(F32)
+            sums = [acc + jnp.where(chosen == b, term, 0.0) for b, acc in enumerate(sums)]
     for b in range(TABLE):
-        value = jnp.where(ids_ref[0, 0] == b, both[0], 0.0) + jnp.where(ids_ref[0, 1] == b, both[1], 0.0)
-        for r in range(per_block):
-            y_send[b * per_block + r] = value[r * rows_y : (r + 1) * rows_y].astype(BF16)
-    for j in range(1, ny):
-        copy = remote(
-            y_send.at[(y + j) % ny], y_recv.at[j - 1], yr_snd.at[j - 1], yr_rcv.at[j - 1], ctx, (y + j) % ny
+        z_all[z, b] = sums[b].astype(BF16)
+    for j in outward(nz):
+        to = (z + j) % nz
+        copy = remote(z_all.at[z], z_all.at[z], z_snd.at[j - 1], z_rcv.at[j - 1], ctx_z(to), y)
+        copy.start()
+        sends.append(copy)
+    for j in outward(nz)[::-1]:
+        frm = (z + nz - j) % nz
+        remote(z_all.at[frm], z_all.at[frm], z_snd.at[j - 1], z_rcv.at[j - 1], ctx_z(frm), y).wait_recv()
+    total = z_all[0].astype(F32)
+    for k in range(1, nz):
+        total += z_all[k].astype(F32)
+    y_all[y] = total.astype(BF16)
+
+    def table_out(kind, yy, xs):
+        return dg_out.at[kind, :, yy, :, pl.ds(pl.multiple_of(xs * wide, HS), wide)]
+
+    for j in outward(ny):
+        to = (y + j) % ny
+        copy = remote(y_all.at[y], y_all.at[y], yg_snd.at[j - 1], yg_rcv.at[j - 1], ctx, to)
+        copy.start()
+        sends.append(copy)
+
+    def to_sibling(src, yy, xs, j, d):
+        copy = remote(src, table_out(c, yy, xs), cg_snd.at[j, d], cg_rcv.at[j, d], sib, y)
+        copy.start()
+        sends.append(copy)
+        pending.append(
+            remote(src, table_out(1 - c, yy, xs), cg_snd.at[j, d], cg_rcv.at[j, d], sib, y)
         )
-        copy.start()
-        sends.append(copy)
-    finish(hx - 1)
-    for j in range(1, ny):
-        remote(y_send.at[y], y_recv.at[j - 1], yr_snd.at[j - 1], yr_rcv.at[j - 1], ctx, y).wait_recv()
-    total = y_send[y].astype(F32)
-    for j in range(1, ny):
-        total += y_recv[j - 1].astype(F32)
-    parts = z_send.shape[0]
-    rows_z = z_send.shape[1]
-    every = nz // parts
-    for k in range(parts):
-        z_send[k] = total[k * rows_z : (k + 1) * rows_z].astype(BF16)
-    is_owner = z % every == 0
-    mine = z // every
-
-    def z_reduce(k, j):
-        return remote(
-            z_send.at[k], z_recv.at[j - 1], zr_snd.at[j - 1], zr_rcv.at[j - 1], ctx_z((z + j) % nz), y
-        )
-
-    def z_gather(j, k):
-        return remote(
-            y_all.at[y, k], y_all.at[y, k], zg_snd.at[j - 1], zg_rcv.at[k], ctx_z((z + j) % nz), y
-        )
-
-    for j in range(1, nz):
-        to = (z + j) % nz
-
-        @pl.when(to % every == 0)
-        def _(j=j, to=to):
-            z_reduce(to // every, j).start()
-
-    @pl.when(is_owner)
-    def _():
-        for j in range(1, nz):
-            z_reduce(0, j).wait_recv()
-        acc = z_send[mine].astype(F32)
-        for j in range(1, nz):
-            acc += z_recv[j - 1].astype(F32)
-        y_all[y, mine] = acc.astype(BF16)
-        for j in range(1, nz):
-            z_gather(j, mine).start()
-
-    for k in range(parts):
-
-        @pl.when(z != k * every)
-        def _(k=k):
-            z_gather(1, k).wait_recv()
-
-    for j in range(1, ny):
-        copy = remote(
-            y_all.at[y], y_all.at[y], yg_snd.at[j - 1], yg_rcv.at[j - 1], ctx, (y + j) % ny
-        )
-        copy.start()
-        sends.append(copy)
-    for j in range(1, ny):
-        frm = (y + ny - j) % ny
-        remote(y_all.at[frm], y_all.at[frm], yg_snd.at[j - 1], yg_rcv.at[j - 1], ctx, y).wait_recv()
-
-    def table_out(xs, kind):
-        return dg_out.at[kind, :, :, :, pl.ds(pl.multiple_of(xs * wide, HS), wide)]
-
-    for j in (2, 1, 3):
-        copy = remote(
-            y_all, table_out(x, c), xg_snd.at[j - 1], xg_rcv.at[j - 1], ctx_x(at_x(j)), y
-        )
-        copy.start()
-        sends.append(copy)
-    copy = pltpu.make_async_copy(y_all, table_out(x, c), xg_loc.at[0])
-    copy.start()
-    locals_out.append(copy)
-
-    def to_sibling(src, xs, j):
-        copy = remote(src, table_out(xs, c), cg_snd.at[j], cg_rcv.at[j], sib, y)
-        copy.start()
-        sends.append(copy)
-        pending.append(remote(src, table_out(xs, 1 - c), cg_snd.at[j], cg_rcv.at[j], sib, y))
-
-    to_sibling(y_all, x, 0)
-    for j in (1, 3, 2):
-        frm = at_x(NX - j)
-        remote(y_all, table_out(frm, c), xg_snd.at[j - 1], xg_rcv.at[j - 1], ctx_x(frm), y).wait_recv()
-        to_sibling(table_out(frm, c), frm, j)
+
+    def spread(d):
+        yy = (y + ny - d) % ny
+        for j in (2, 1, 3):
+            copy = remote(
+                y_all.at[yy],
+                table_out(c, yy, x),
+                xg_snd.at[j - 1, d],
+                xg_rcv.at[j - 1, d],
+                ctx_x(at_x(j)),
+                y,
+            )
+            copy.start()
+            sends.append(copy)
+        to_sibling(y_all.at[yy], yy, x, 0, d)
+        copy = pltpu.make_async_copy(y_all.at[yy], table_out(c, yy, x), xg_loc.at[d])
+        copy.start()
+        locals_out.append(copy)
+
+    def pass_on(d):
+        yy = (y + ny - d) % ny
+        for j in (1, 3, 2):
+            frm = at_x(NX - j)
+            remote(
+                y_all.at[yy],
+                table_out(c, yy, frm),
+                xg_snd.at[j - 1, d],
+                xg_rcv.at[j - 1, d],
+                ctx_x(frm),
+                y,
+            ).wait_recv()
+            to_sibling(table_out(c, yy, frm), yy, frm, j, d)
+
+    spread(0)
+    before = [0]
+    near = outward(ny)[::-1]
+    for start in range(0, len(near), 2):
+        group = near[start : start + 2]
+        for d in group:
+            frm = (y + ny - d) % ny
+            remote(
+                y_all.at[frm], y_all.at[frm], yg_snd.at[d - 1], yg_rcv.at[d - 1], ctx, frm
+            ).wait_recv()
+            spread(d)
+        for d in before:
+            pass_on(d)
+        before = group
+    for d in before:
+        pass_on(d)
 
     for copy in pending:
         copy.wait_recv()
@@ -473,16 +497,28 @@
         copy.wait()
     for copy in sends:
         copy.wait_send()
-    for j in range(1, nz):
-        to = (z + j) % nz
-
-        @pl.when(to % every == 0)
-        def _(j=j):
-            z_reduce(0, j).wait_send()
-
-        @pl.when(is_owner)
-        def _(j=j):
-            z_gather(j, mine).wait_send()
+
+
+def last_step(dq_in, dk_in, dv_in, dg_in, dq_out, dk_out, dv_out, dg_out, narrow, full, moved, got, put):
+    moves = []
+    for i, (src, dst_ref) in enumerate(((dq_in, dq_out), (dk_in, dk_out), (dv_in, dv_out))):
+        copy = pltpu.make_async_copy(src, dst_ref, moved.at[i])
+        copy.start()
+        moves.append(copy)
+    parts = narrow.shape[0]
+    loads = []
+    for i in range(parts):
+        copy = pltpu.make_async_copy(dg_in.at[i // TABLE, i % TABLE], narrow.at[i], got.at[i])
+        copy.start()
+        loads.append(copy)
+    for i in range(parts):
+        loads[i].wait()
+        full[i] = narrow[i].astype(F32)
+        copy = pltpu.make_async_copy(full.at[i], dg_out.at[i // TABLE, i % TABLE], put.at[i])
+        copy.start()
+        moves.append(copy)
+    for copy in moves:
+        copy.wait()
 
 
 def on_device(nz, ny, query, key, value, dout, glob_keys, glob_values, glob_ids, rand_blocks):
@@ -490,15 +526,13 @@
     hx = heads // NX
     hd = query.shape[2]
     wide = hx * HS
-    rows_y = TABLE * BLK // ny
-    parts = 4
-    rows_z = rows_y // parts
+    rows_y = BLK // ny
     blocks = [a.reshape(2, BLK, hd) for a in (query, key, value, dout)]
     rand = jnp.transpose(rand_blocks, (2, 0, 1))
     vm = pltpu.VMEM
     dma = pltpu.SemaphoreType.DMA
     out = jax.ShapeDtypeStruct((2, BLK, hd), BF16)
-    anywhere = pl.BlockSpec(memory_space=pl.ANY)
+    anywhere = pl.BlockSpec(memory_space=pltpu.HBM)
     scalars = pl.BlockSpec(memory_space=pltpu.SMEM)
     scratch = [
         vm((hx, 2 * NX, 2, BLK, HS), BF16),
@@ -516,11 +550,11 @@
         vm((2, 2, BLK, wide), F32),
         vm((2, 2, BLK, wide), BF16),
         vm((2, BLK, wide), BF16),
-        vm((ny, rows_y, wide), BF16),
-        vm((max(ny - 1, 1), rows_y, wide), BF16),
-        vm((parts, rows_z, wide), BF16),
-        vm((max(nz - 1, 1), rows_z, wide), BF16),
-        vm((ny, parts, rows_z, wide), BF16),
+        vm((ny, 2, rows_y, HS), jnp.int32),
+        vm((ny, 2, rows_y, wide), BF16),
+        vm((ny, 2, rows_y, wide), BF16),
+        vm((nz, TABLE, rows_y, wide), BF16),
+        vm((ny, TABLE, rows_y, wide), BF16),
         dma((hx, 4)),
         dma((hx, 4, 3)),
         dma((hx, 4, 3)),
@@ -539,30 +573,47 @@
         dma((1,)),
         dma((ny,)),
         dma((ny,)),
+        dma((ny,)),
+        dma((ny,)),
         dma((nz,)),
         dma((nz,)),
-        dma((nz,)),
-        dma((parts,)),
         dma((ny,)),
         dma((ny,)),
-        dma((1,)),
-        dma((3,)),
-        dma((3,)),
-        dma((4,)),
-        dma((4,)),
+        dma((ny,)),
+        dma((3, ny)),
+        dma((3, ny)),
+        dma((4, ny)),
+        dma((4, ny)),
     ]
     dq, dk, dv, dg = pl.pallas_call(
         functools.partial(body, nz, ny, hx),
-        out_shape=(out, out, out, jax.ShapeDtypeStruct((2, ny, parts, rows_z, hd), BF16)),
+        out_shape=(out, out, out, jax.ShapeDtypeStruct((2, TABLE, ny, rows_y, hd), BF16)),
         in_specs=[scalars, scalars] + [anywhere] * 6,
         out_specs=(anywhere,) * 4,
         scratch_shapes=scratch,
         compiler_params=pltpu.CompilerParams(
-            collective_id=0, has_side_effects=True, vmem_limit_bytes=48 * 1024 * 1024
+            collective_id=0, has_side_effects=True, vmem_limit_bytes=60 * 1024 * 1024
         ),
     )(glob_ids, rand, *blocks, glob_keys, glob_values)
+    rows = jax.ShapeDtypeStruct((1, 2 * BLK, hd), BF16)
     dq, dk, dv = (a.reshape(1, 2 * BLK, hd) for a in (dq, dk, dv))
-    return dq, dk, dv, dg.reshape(2, TABLE, BLK, hd).astype(F32)
+    parts = 2 * TABLE
+    return tuple(
+        pl.pallas_call(
+            last_step,
+            out_shape=(rows, rows, rows, jax.ShapeDtypeStruct((2, TABLE, BLK, hd), F32)),
+            in_specs=[anywhere] * 4,
+            out_specs=(anywhere,) * 4,
+            scratch_shapes=[
+                vm((parts, BLK, hd), BF16),
+                vm((parts, BLK, hd), F32),
+                dma((3,)),
+                dma((parts,)),
+                dma((parts,)),
+            ],
+            compiler_params=pltpu.CompilerParams(vmem_limit_bytes=60 * 1024 * 1024),
+        )(dq, dk, dv, dg.reshape(2, TABLE, BLK, hd))
+    )
 
 
 def solution(mesh):

time: 84.5 us -> 99 us (1.17)
  Pallas kernels: 72.5 us -> 98.1 us
  local copies, waits for them, and re-layouts: 9.37 us -> 0 us
  other arithmetic: 1.57 us -> 0 us
    pallas_call x0 -> x1, Pallas kernels: none -> 25.1 us  [on_device(): pl.pallas_call(last_step, out_shape=(rows, rows, rows, jax.ShapeDtypeStru...]
    unnamed x19 -> x0, local copies, waits for them, and re-layouts: 9.37 us -> none
    convert_element_type x1 -> x0, other arithmetic: 1.57 us -> none  [on_device(): return (dq, dk, dv, dg.reshape(2, TABLE, BLK, hd).astype(F32))]
where the time goes in v2:
time: 99 us; the launch traced here: 98.7 us
  Pallas kernels  98.1 us (99%)
    pallas_call x1, Pallas kernels, on_device(): pl.pallas_call(functools.partial(body, nz, ny, hx), out_shape=(out, out,...  73 us
    pallas_call x1, Pallas kernels, on_device(): pl.pallas_call(last_step, out_shape=(rows, rows, rows, jax.ShapeDtypeStru...  25.1 us

profile of v2, /device:TPU:1, one launch (start us, length us, event | category | flops | bytes accessed | tf_op | source)
XLA Modules:
  0.0 98.7 jit_solution(2193914626988928810)
XLA Ops:
  0.6 73.0 %shard_map.111 = (bf16[2,64,1024]{2,1,0:T(8,128)(2,1)}, bf16[2,64,1024]{2,1,0:T(8,128)(2,1)}, bf16[2,64,1024]{2,1,0:T(8,128)(2,1)}, bf16[2,4,8,8,1024]{4,3,2,1,0:T(8,128)(2,1)}) custom-call(s32[1,2]{1,0:T(1,128)} %ids_ref.1, s32[3,8,192]{2,1,0:T(8,128)} %bitcast.17, bf16[2,64,1024]{2,1,0:T(8,128)(2,1)} %bitcast.10, bf16[2,64,1024]{2,1,0:T(8,128)(2,1)} %bitcast.11, ...), custom_call_target="tpu_custom_call" | custom-call | tf_op jit(solution)/shard_map/pallas_call | solution.py:588
  73.6 25.1 %shard_map.112 = (bf16[1,128,1024]{2,1,0:T(8,128)(2,1)}, bf16[1,128,1024]{2,1,0:T(8,128)(2,1)}, bf16[1,128,1024]{2,1,0:T(8,128)(2,1)}, f32[2,4,64,1024]{3,2,1,0:T(8,128)}) custom-call(bf16[1,128,1024]{2,1,0:T(8,128)(2,1)} %bitcast.14, bf16[1,128,1024]{2,1,0:T(8,128)(2,1)} %bitcast.15, bf16[1,128,1024]{2,1,0:T(8,128)(2,1)} %bitcast.16, ...), custom_call_target="tpu_custom_call" | custom-call | tf_op jit(solution)/shard_map/pallas_call | solution.py:602

commit v3 on v2

--- a/solution.py
+++ b/solution.py
@@ -70,6 +70,7 @@
     y_recv,
     z_all,
     y_all,
+    table,
     in_loc,
     in_snd,
     in_rcv,
@@ -95,10 +96,12 @@
     yg_snd,
     yg_rcv,
     xg_loc,
+    t_out,
     xg_snd,
     xg_rcv,
     cg_snd,
     cg_rcv,
+    word,
 ):
     ring = nz * 2
     ctx = lax.axis_index("ctx")
@@ -135,8 +138,8 @@
         )
 
     tab_copies = []
-    for t, table in enumerate((gk_in, gv_in)):
-        copy = pltpu.make_async_copy(table.at[:, :, pl.ds(own_cols, wide)], tab.at[t], tab_sem.at[t])
+    for t, blocks in enumerate((gk_in, gv_in)):
+        copy = pltpu.make_async_copy(blocks.at[:, :, pl.ds(own_cols, wide)], tab.at[t], tab_sem.at[t])
         copy.start()
         tab_copies.append(copy)
 
@@ -156,14 +159,30 @@
             copy.start()
             local_in[h, t] = copy
 
+    beside = [(ctx, (y + 1) % ny), (ctx, (y + ny - 1) % ny)]
+    beside += [(ctx_z((z + 1) % nz), y), (ctx_z((z + nz - 1) % nz), y)]
+
+    def pass_word(k):
+        for i, (to_ctx, to_y) in enumerate(beside):
+            if k <= (ny if i < 2 else nz) // 2 - 1:
+                pl.semaphore_signal(
+                    word.at[k - 1, i], inc=1, device_id={"ctx": to_ctx, "dp": to_y}, device_id_type=MESH
+                )
+
+    def hear_word(k):
+        for i in range(4):
+            if k <= (ny if i < 2 else nz) // 2 - 1:
+                pl.semaphore_wait(word.at[k - 1, i], 1)
+        pass_word(k + 1)
+
     barrier = pltpu.get_barrier_semaphore()
     partners = [(ctx_x(at_x(j)), y) for j in range(1, NX)]
     partners += [(sib, y), (far, y)]
-    partners += [(ctx, (y + j) % ny) for j in range(1, ny)]
-    partners += [(ctx_z((z + j) % nz), y) for j in range(1, nz)]
+    partners += beside
     for to_ctx, to_y in partners:
         pl.semaphore_signal(barrier, inc=1, device_id={"ctx": to_ctx, "dp": to_y}, device_id_type=MESH)
     pl.semaphore_wait(barrier, len(partners))
+    pass_word(1)
 
     sends = []
 
@@ -188,24 +207,16 @@
                 land(h, t, frm), land(h, t, frm), in_snd.at[h, t, j - 1], in_rcv.at[h, t, j - 1], ctx_x(frm), y
             ).wait_recv()
 
-    for pair in ((0, 1), (2, 3)):
-        for h in range(hx):
-            for t in pair:
-                for j in (2, 1, 3):
-                    send_in(h, t, j)
+    for h in range(hx):
+        for t in range(2):
+            for j in (2, 1, 3):
+                send_in(h, t, j)
+        for j in (1, 3, 2):
+            for t in range(2, 4):
+                send_in(h, t, j)
 
     for s in range(2):
         ids_all[y, s] = jnp.full((BLK // ny, HS), ids_ref[0, s], jnp.int32)
-    id_waits = []
-    for j in range(1, ny):
-        to, frm = (y + j) % ny, (y + ny - j) % ny
-        copy = remote(ids_all.at[y], ids_all.at[y], id_snd.at[j - 1], id_rcv.at[j - 1], ctx, to)
-        copy.start()
-        sends.append(copy)
-        id_waits.append(
-            remote(ids_all.at[frm], ids_all.at[frm], id_snd.at[j - 1], id_rcv.at[j - 1], ctx, frm)
-        )
-
     for copy in tab_copies:
         copy.wait()
     for h in range(hx):
@@ -214,7 +225,9 @@
                 gsel[h, t, s] = tab[t, ids_ref[0, s], :, h * HS : (h + 1) * HS]
 
     edge_copies = {}
-    for h in range(hx):
+
+
+    def send_edges(h):
         wait_in(h, 0)
         wait_in(h, 1)
         for way, to in ((0, up), (1, low)):
@@ -236,7 +249,18 @@
         lane = lax.broadcasted_iota(jnp.int32, (1, 2 * BLK), 1)
         half = lane // BLK
 
-        def span(xq, carry):
+        def span(i, carry):
+            off = jnp.where(i == 1, NX - 1, jnp.where(i == 0, 0, i - 1))
+            xq = (x + off) % NX
+            sem = jnp.where(i == 1, 0, jnp.where(i == 2, 2, 1))
+
+            @pl.when(i > 0)
+            def _():
+                for t in range(2, 4):
+                    remote(
+                        land(h, t, xq), land(h, t, xq), in_snd.at[h, t, sem], in_rcv.at[h, t, sem], ctx_x(xq), y
+                    ).wait_recv()
+
             q = qd[h, xq].reshape(2 * BLK, HS)
             g = qd[h, NX + xq].reshape(2 * BLK, HS)
             i_low = (xq + NX - seam_low) % NX
@@ -305,13 +329,30 @@
             edge_s[h, 1, NX + i_up] = dv_edge[BLK:]
             return carry
 
+        for t in range(2, 4):
+            local_in[h, t].wait()
         lax.fori_loop(0, NX, span, 0)
+
+    last_row = NX * 2 * BLK
+
+    def tables(h):
         for t, lists in ((0, dst), (1, pt)):
             rows = qd[h, t * NX : (t + 1) * NX].reshape(NX * 2 * BLK, HS)
-            grad = dot_nn(lists[...], rows)
-            dkv[h, t * NX : (t + 1) * NX] = grad[: NX * 2 * BLK].reshape(NX, 2, BLK, HS)
-            gp[t, :, :, h * HS : (h + 1) * HS] = grad[NX * 2 * BLK :].reshape(2, BLK, HS)
-
+            grad = dot_nn(lists[last_row:], rows).reshape(2, BLK, HS)
+            gp[h, t] = grad
+            gpb[h, t] = grad.astype(BF16)
+        copy = remote(gpb.at[h, 1 - c], g_core.at[h], c_snd.at[h], c_rcv.at[h], sib, y)
+        copy.start()
+        core_copies[h] = copy
+        sends.append(copy)
+
+    def mains(h):
+        for t, lists in ((0, dst), (1, pt)):
+            rows = qd[h, t * NX : (t + 1) * NX].reshape(NX * 2 * BLK, HS)
+            grad = dot_nn(lists[:last_row], rows)
+            dkv[h, t * NX : (t + 1) * NX] = grad.reshape(NX, 2, BLK, HS)
+
+    core_copies = {}
     back_copies = {}
     pending = []
     locals_out = []
@@ -337,7 +378,7 @@
         copy.start()
         locals_out.append(copy)
 
-    def after(h):
+    def send_back(h):
         for way, to in ((0, low), (1, up)):
             copy = remote(
                 edge_s.at[h, way], edge_r.at[h, way], b_snd.at[h, way], b_rcv.at[h, way], to, y
@@ -345,6 +386,8 @@
             copy.start()
             back_copies[h, way] = copy
             sends.append(copy)
+
+    def send_dq(h):
         send_out(
             dq_out,
             lambda xs: dqs.at[h, xs],
@@ -372,63 +415,106 @@
                 dkv_loc.at[h, t],
             )
 
+    rows_y = BLK // ny
+
+    def y_start(h):
+        core_copies[h].wait_recv()
+        for s in range(2):
+            both = (gp[h, c, s] + g_core[h, s].astype(F32)).astype(BF16)
+            for r in range(ny):
+                y_send[h, r, s] = both[r * rows_y : (r + 1) * rows_y]
+        for j in outward(ny):
+            to = (y + j) % ny
+            copy = remote(
+                y_send.at[h, to], y_recv.at[h, y], yr_snd.at[h, j - 1], yr_rcv.at[h, j - 1], ctx, to
+            )
+            copy.start()
+            sends.append(copy)
+        y_recv[h, y] = y_send[h, y]
+
+    def z_start(h):
+        for j in outward(ny)[::-1]:
+            frm = (y + ny - j) % ny
+            remote(
+                y_send.at[h, y], y_recv.at[h, frm], yr_snd.at[h, j - 1], yr_rcv.at[h, j - 1], ctx, frm
+            ).wait_recv()
+        sums = [jnp.zeros((rows_y, HS), F32) for _ in range(TABLE)]
+        for src in range(ny):
+            for s in range(2):
+                chosen = ids_all[src, s]
+                term = y_recv[h, src, s].astype(F32)
+                sums = [acc + jnp.where(chosen == b, term, 0.0) for b, acc in enumerate(sums)]
+        for b in range(TABLE):
+            z_all[h, z, b] = sums[b].astype(BF16)
+        for j in outward(nz):
+            to = (z + j) % nz
+            copy = remote(
+                z_all.at[h, z], z_all.at[h, z], z_snd.at[h, j - 1], z_rcv.at[h, j - 1], ctx_z(to), y
+            )
+            copy.start()
+            sends.append(copy)
+
+    def z_end(h):
+        for j in outward(nz)[::-1]:
+            frm = (z + nz - j) % nz
+            remote(
+                z_all.at[h, frm], z_all.at[h, frm], z_snd.at[h, j - 1], z_rcv.at[h, j - 1], ctx_z(frm), y
+            ).wait_recv()
+        total = z_all[h, 0].astype(F32)
+        for k in range(1, nz):
+            total += z_all[h, k].astype(F32)
+        y_all[y, h] = total.astype(BF16)
+
+    id_waits = []
+
+    def send_ids():
+        for j in range(1, ny):
+            to, frm = (y + j) % ny, (y + ny - j) % ny
+            copy = remote(ids_all.at[y], ids_all.at[y], id_snd.at[j - 1], id_rcv.at[j - 1], ctx, to)
+            copy.start()
+            sends.append(copy)
+            id_waits.append(
+                remote(ids_all.at[frm], ids_all.at[frm], id_snd.at[j - 1], id_rcv.at[j - 1], ctx, frm)
+            )
+
+    last = hx - 1
+    send_edges(0)
+    hear_word(1)
     for h in range(hx):
-        wait_in(h, 2)
-        wait_in(h, 3)
         for way in range(2):
             edge_copies[h, way].wait_recv()
+        if h == 0:
+            hear_word(2)
         compute(h)
-        after(h)
-
-    gpb[...] = gp[...].astype(BF16)
-    core_copy = remote(gpb.at[1 - c], g_core, c_snd.at[0], c_rcv.at[0], sib, y)
-    core_copy.start()
-    sends.append(core_copy)
-    for h in range(hx - 1):
-        finish(h)
-    core_copy.wait_recv()
-    rows_y = BLK // ny
-    for s in range(2):
-        both = (gp[c, s] + g_core[s].astype(F32)).astype(BF16)
-        for r in range(ny):
-            y_send[r, s] = both[r * rows_y : (r + 1) * rows_y]
-    for j in outward(ny):
-        to = (y + j) % ny
-        copy = remote(y_send.at[to], y_recv.at[y], yr_snd.at[j - 1], yr_rcv.at[j - 1], ctx, to)
-        copy.start()
-        sends.append(copy)
-    y_recv[y] = y_send[y]
-    finish(hx - 1)
+        if h == 0:
+            hear_word(3)
+            send_ids()
+        tables(h)
+        send_back(h)
+        if h < last:
+            mains(h)
+            send_edges(h + 1)
+            hear_word(4)
+            y_start(h)
+    hear_word(5)
     for copy in id_waits:
         copy.wait_recv()
+    for h in range(last):
+        z_start(h)
+    mains(last)
+    y_start(last)
+    for h in range(hx):
+        send_dq(h)
+    for h in range(hx):
+        finish(h)
+    z_start(last)
+    for h in range(hx):
+        z_end(h)
+
+    def table_out(kind, yy, xs):
+        return table.at[kind, xs, yy]
+
     for j in outward(ny)[::-1]:
-        frm = (y + ny - j) % ny
-        remote(y_send.at[y], y_recv.at[frm], yr_snd.at[j - 1], yr_rcv.at[j - 1], ctx, frm).wait_recv()
-    sums = [jnp.zeros((rows_y, wide), F32) for _ in range(TABLE)]
-    for src in range(ny):
-        for s in range(2):
-            chosen = jnp.concatenate([ids_all[src, s]] * hx, axis=1)
-            term = y_recv[src, s].astype(F32)
-            sums = [acc + jnp.where(chosen == b, term, 0.0) for b, acc in enumerate(sums)]
-    for b in range(TABLE):
-        z_all[z, b] = sums[b].astype(BF16)
-    for j in outward(nz):
-        to = (z + j) % nz
-        copy = remote(z_all.at[z], z_all.at[z], z_snd.at[j - 1], z_rcv.at[j - 1], ctx_z(to), y)
-        copy.start()
-        sends.append(copy)
-    for j in outward(nz)[::-1]:
-        frm = (z + nz - j) % nz
-        remote(z_all.at[frm], z_all.at[frm], z_snd.at[j - 1], z_rcv.at[j - 1], ctx_z(frm), y).wait_recv()
-    total = z_all[0].astype(F32)
-    for k in range(1, nz):
-        total += z_all[k].astype(F32)
-    y_all[y] = total.astype(BF16)
-
-    def table_out(kind, yy, xs):
-        return dg_out.at[kind, :, yy, :, pl.ds(pl.multiple_of(xs * wide, HS), wide)]
-
-    for j in outward(ny):
         to = (y + j) % ny
         copy = remote(y_all.at[y], y_all.at[y], yg_snd.at[j - 1], yg_rcv.at[j - 1], ctx, to)
         copy.start()
@@ -491,33 +577,47 @@
     for d in before:
         pass_on(d)
 
+    for copy in locals_out:
+        copy.wait()
+    final = [pltpu.make_async_copy(table.at[k], dg_out.at[k], t_out.at[i]) for i, k in enumerate((c, 1 - c))]
+    final[0].start()
     for copy in pending:
         copy.wait_recv()
-    for copy in locals_out:
-        copy.wait()
+    final[1].start()
     for copy in sends:
         copy.wait_send()
-
-
-def last_step(dq_in, dk_in, dv_in, dg_in, dq_out, dk_out, dv_out, dg_out, narrow, full, moved, got, put):
-    moves = []
-    for i, (src, dst_ref) in enumerate(((dq_in, dq_out), (dk_in, dk_out), (dv_in, dv_out))):
-        copy = pltpu.make_async_copy(src, dst_ref, moved.at[i])
-        copy.start()
-        moves.append(copy)
+    for copy in final:
+        copy.wait()
+
+
+def last_step(dq_in, dk_in, dv_in, dg_in, dq_out, dk_out, dv_out, dg_out, rows, narrow, full, got, put):
     parts = narrow.shape[0]
     loads = []
     for i in range(parts):
-        copy = pltpu.make_async_copy(dg_in.at[i // TABLE, i % TABLE], narrow.at[i], got.at[i])
-        copy.start()
-        loads.append(copy)
+        loads.append(
+            pltpu.make_async_copy(dg_in.at[i // NX, i % NX], narrow.at[i], got.at[i])
+        )
+    for i, src in enumerate((dq_in, dk_in, dv_in)):
+        loads.append(pltpu.make_async_copy(src.at[0], rows.at[i], got.at[parts + i]))
+    for copy in loads:
+        copy.start()
+    stores = []
     for i in range(parts):
         loads[i].wait()
-        full[i] = narrow[i].astype(F32)
-        copy = pltpu.make_async_copy(full.at[i], dg_out.at[i // TABLE, i % TABLE], put.at[i])
-        copy.start()
-        moves.append(copy)
-    for copy in moves:
+        for h in range(narrow.shape[2]):
+            for b in range(TABLE):
+                rows_b = narrow[i, :, h, b].astype(F32).reshape(BLK, HS)
+                full[i, b, :, h * HS : (h + 1) * HS] = rows_b
+        cols = pl.ds(i % NX * full.shape[3], full.shape[3])
+        copy = pltpu.make_async_copy(full.at[i], dg_out.at[i // NX, :, :, cols], put.at[i])
+        copy.start()
+        stores.append(copy)
+    for i, dst_ref in enumerate((dq_out, dk_out, dv_out)):
+        loads[parts + i].wait()
+        copy = pltpu.make_async_copy(rows.at[i], dst_ref.at[0], put.at[parts + i])
+        copy.start()
+        stores.append(copy)
+    for copy in stores:
         copy.wait()
 
 
@@ -547,14 +647,15 @@
         vm((hx, 2 * NX, 2, BLK, HS), BF16),
         vm((hx, 2, 2 * NX, BLK, HS), BF16),
         vm((hx, 2, 2 * NX, BLK, HS), BF16),
-        vm((2, 2, BLK, wide), F32),
-        vm((2, 2, BLK, wide), BF16),
-        vm((2, BLK, wide), BF16),
+        vm((hx, 2, 2, BLK, HS), F32),
+        vm((hx, 2, 2, BLK, HS), BF16),
+        vm((hx, 2, BLK, HS), BF16),
         vm((ny, 2, rows_y, HS), jnp.int32),
-        vm((ny, 2, rows_y, wide), BF16),
-        vm((ny, 2, rows_y, wide), BF16),
-        vm((nz, TABLE, rows_y, wide), BF16),
-        vm((ny, TABLE, rows_y, wide), BF16),
+        vm((hx, ny, 2, rows_y, HS), BF16),
+        vm((hx, ny, 2, rows_y, HS), BF16),
+        vm((hx, nz, TABLE, rows_y, HS), BF16),
+        vm((ny, hx, TABLE, rows_y, HS), BF16),
+        vm((2, NX, ny, hx, TABLE, rows_y, HS), BF16),
         dma((hx, 4)),
         dma((hx, 4, 3)),
         dma((hx, 4, 3)),
@@ -569,25 +670,27 @@
         dma((hx, 2)),
         dma((hx, 2, 3)),
         dma((hx, 2, 3)),
-        dma((1,)),
-        dma((1,)),
+        dma((hx,)),
+        dma((hx,)),
+        dma((ny,)),
+        dma((ny,)),
+        dma((hx, ny)),
+        dma((hx, ny)),
+        dma((hx, nz)),
+        dma((hx, nz)),
         dma((ny,)),
         dma((ny,)),
         dma((ny,)),
-        dma((ny,)),
-        dma((nz,)),
-        dma((nz,)),
-        dma((ny,)),
-        dma((ny,)),
-        dma((ny,)),
+        dma((2,)),
         dma((3, ny)),
         dma((3, ny)),
         dma((4, ny)),
         dma((4, ny)),
+        pltpu.SemaphoreType.REGULAR((max(ny, nz) // 2, 4)),
     ]
     dq, dk, dv, dg = pl.pallas_call(
         functools.partial(body, nz, ny, hx),
-        out_shape=(out, out, out, jax.ShapeDtypeStruct((2, TABLE, ny, rows_y, hd), BF16)),
+        out_shape=(out, out, out, jax.ShapeDtypeStruct((2, NX, ny, hx, TABLE, rows_y, HS), BF16)),
         in_specs=[scalars, scalars] + [anywhere] * 6,
         out_specs=(anywhere,) * 4,
         scratch_shapes=scratch,
@@ -597,7 +700,7 @@
     )(glob_ids, rand, *blocks, glob_keys, glob_values)
     rows = jax.ShapeDtypeStruct((1, 2 * BLK, hd), BF16)
     dq, dk, dv = (a.reshape(1, 2 * BLK, hd) for a in (dq, dk, dv))
-    parts = 2 * TABLE
+    parts = 2 * NX
     return tuple(
         pl.pallas_call(
             last_step,
@@ -605,14 +708,14 @@
             in_specs=[anywhere] * 4,
             out_specs=(anywhere,) * 4,
             scratch_shapes=[
-                vm((parts, BLK, hd), BF16),
-                vm((parts, BLK, hd), F32),
-                dma((3,)),
-                dma((parts,)),
-                dma((parts,)),
+                vm((3, 2 * BLK, hd), BF16),
+                vm((parts, ny, hx, TABLE, rows_y, HS), BF16),
+                vm((parts, TABLE, BLK, wide), F32),
+                dma((parts + 3,)),
+                dma((parts + 3,)),
             ],
             compiler_params=pltpu.CompilerParams(vmem_limit_bytes=60 * 1024 * 1024),
-        )(dq, dk, dv, dg.reshape(2, TABLE, BLK, hd))
+        )(dq, dk, dv, dg)
     )
 
 

time: 99 us -> 73.1 us (0.74)
  Pallas kernels: 98.1 us -> 72.2 us
    pallas_call x1, Pallas kernels: 25.1 us -> 2.68 us  [on_device(): pl.pallas_call(last_step, out_shape=(rows, rows, rows, jax.ShapeDtypeStru...]
    pallas_call x1, Pallas kernels: 73 us -> 69.5 us  [on_device(): pl.pallas_call(functools.partial(body, nz, ny, hx), out_shape=(out, out,...]
where the time goes in v3:
time: 73.1 us; the launch traced here: 72.8 us
  Pallas kernels  72.2 us (99%)
    pallas_call x1, Pallas kernels, on_device(): pl.pallas_call(functools.partial(body, nz, ny, hx), out_shape=(out, out,...  69.5 us
    pallas_call x1, Pallas kernels, on_device(): pl.pallas_call(last_step, out_shape=(rows, rows, rows, jax.ShapeDtypeStru...  2.68 us

profile of v3, /device:TPU:1, one launch (start us, length us, event | category | flops | bytes accessed | tf_op | source)
XLA Modules:
  0.0 72.8 jit_solution(3230289064279510859)
XLA Ops:
  0.6 69.5 %shard_map.111 = (bf16[2,64,1024]{2,1,0:T(8,128)(2,1)}, bf16[2,64,1024]{2,1,0:T(8,128)(2,1)}, bf16[2,64,1024]{2,1,0:T(8,128)(2,1)}, bf16[2,4,8,2,4,8,128]{6,5,4,3,2,1,0:T(8,128)(2,1)}) custom-call(s32[1,2]{1,0:T(1,128)} %ids_ref.1, s32[3,8,192]{2,1,0:T(8,128)} %bitcast.15, bf16[2,64,1024]{2,1,0:T(8,128)(2,1)} %bitcast.8, bf16[2,64,1024]{2,1,0:T(8,128)(2,1)} %bitcast.9, ...), custom_call_target="tpu_custom_call" | custom-call | tf_op jit(solution)/shard_map/pallas_call | solution.py:691
  70.1 2.7 %shard_map.112 = (bf16[1,128,1024]{2,1,0:T(8,128)(2,1)}, bf16[1,128,1024]{2,1,0:T(8,128)(2,1)}, bf16[1,128,1024]{2,1,0:T(8,128)(2,1)}, f32[2,4,64,1024]{3,2,1,0:T(8,128)}) custom-call(bf16[1,128,1024]{2,1,0:T(8,128)(2,1)} %bitcast.12, bf16[1,128,1024]{2,1,0:T(8,128)(2,1)} %bitcast.13, bf16[1,128,1024]{2,1,0:T(8,128)(2,1)} %bitcast.14, ...), custom_call_target="tpu_custom_call" | custom-call | tf_op jit(solution)/shard_map/pallas_call | solution.py:705

commit v4 on v3

--- a/solution.py
+++ b/solution.py
@@ -38,8 +38,8 @@
     nz,
     ny,
     hx,
-    ids_ref,
-    rand_ref,
+    ids_in,
+    rand_in,
     q_in,
     k_in,
     v_in,
@@ -102,6 +102,9 @@
     cg_snd,
     cg_rcv,
     word,
+    ids_ref,
+    rand_ref,
+    scalar_sem,
 ):
     ring = nz * 2
     ctx = lax.axis_index("ctx")
@@ -137,6 +140,11 @@
             device_id_type=MESH,
         )
 
+    scalar_copies = []
+    for i, (src, dst_ref) in enumerate(((ids_in, ids_ref), (rand_in, rand_ref))):
+        copy = pltpu.make_async_copy(src, dst_ref, scalar_sem.at[i])
+        copy.start()
+        scalar_copies.append(copy)
     tab_copies = []
     for t, blocks in enumerate((gk_in, gv_in)):
         copy = pltpu.make_async_copy(blocks.at[:, :, pl.ds(own_cols, wide)], tab.at[t], tab_sem.at[t])
@@ -211,9 +219,13 @@
         for t in range(2):
             for j in (2, 1, 3):
                 send_in(h, t, j)
+    for h in range(hx):
         for j in (1, 3, 2):
             for t in range(2, 4):
                 send_in(h, t, j)
+
+    for copy in scalar_copies:
+        copy.wait()
 
     for s in range(2):
         ids_all[y, s] = jnp.full((BLK // ny, HS), ids_ref[0, s], jnp.int32)
@@ -267,9 +279,9 @@
             i_up = (xq + seam_up) % NX
             k_edge = jnp.concatenate([edge[h, 0, i_low], edge[h, 1, i_up]], axis=0)
             v_edge = jnp.concatenate([edge[h, 0, NX + i_low], edge[h, 1, NX + i_up]], axis=0)
-            s_main = dot_nt(k_main, q) * scaling
-            s_tab = dot_nt(k_tab, q) * scaling
-            s_edge = dot_nt(k_edge, q) * scaling
+            s_main = dot_nt(k_main, q)
+            s_tab = dot_nt(k_tab, q)
+            s_edge = dot_nt(k_edge, q)
             block = 2 * (xq * ring + pos)
             pieces = []
             for xs in range(NX):
@@ -293,7 +305,7 @@
                 pieces.append(jnp.where(keep, s_edge[b * BLK : (b + 1) * BLK], -1e30))
             top = functools.reduce(jnp.maximum, pieces)
             top = jnp.max(top, axis=0, keepdims=True)
-            exps = [jnp.exp(piece - top) for piece in pieces]
+            exps = [jnp.exp2((piece - top) * (scaling * math.log2(math.e))) for piece in pieces]
             total = jnp.sum(functools.reduce(jnp.add, exps), axis=0, keepdims=True)
             inverse = 1.0 / total
             d_main = dot_nt(v_main, g)
@@ -310,23 +322,9 @@
             grads = [
                 (p * (d - row_dot) * scaling).astype(BF16) for p, d in zip(probs, d_pieces)
             ]
-            p_list = jnp.concatenate(probs_b[:10], axis=0)
-            g_list = jnp.concatenate(grads[:10], axis=0)
             cols = pl.ds(pl.multiple_of(xq * 2 * BLK, 2 * BLK), 2 * BLK)
-            pt[:, cols] = p_list
-            dst[:, cols] = g_list
-            g_edge = jnp.concatenate(grads[10:], axis=0)
-            p_edge = jnp.concatenate(probs_b[10:], axis=0)
-            dq = dot_tn(g_list[: NX * 2 * BLK], k_main)
-            dq += dot_tn(g_list[NX * 2 * BLK :], k_tab)
-            dq += dot_tn(g_edge, k_edge)
-            dqs[h, xq] = dq.astype(BF16).reshape(2, BLK, HS)
-            dk_edge = dot_nn(g_edge, q).astype(BF16)
-            dv_edge = dot_nn(p_edge, g).astype(BF16)
-            edge_s[h, 0, i_low] = dk_edge[:BLK]
-            edge_s[h, 1, i_up] = dk_edge[BLK:]
-            edge_s[h, 0, NX + i_low] = dv_edge[:BLK]
-            edge_s[h, 1, NX + i_up] = dv_edge[BLK:]
+            pt[:, cols] = jnp.concatenate(probs_b, axis=0)
+            dst[:, cols] = jnp.concatenate(grads, axis=0)
             return carry
 
         for t in range(2, 4):
@@ -334,11 +332,12 @@
         lax.fori_loop(0, NX, span, 0)
 
     last_row = NX * 2 * BLK
+    tab_row = last_row + 2 * BLK
 
     def tables(h):
         for t, lists in ((0, dst), (1, pt)):
             rows = qd[h, t * NX : (t + 1) * NX].reshape(NX * 2 * BLK, HS)
-            grad = dot_nn(lists[last_row:], rows).reshape(2, BLK, HS)
+            grad = dot_nn(lists[last_row:tab_row], rows).reshape(2, BLK, HS)
             gp[h, t] = grad
             gpb[h, t] = grad.astype(BF16)
         copy = remote(gpb.at[h, 1 - c], g_core.at[h], c_snd.at[h], c_rcv.at[h], sib, y)
@@ -346,7 +345,25 @@
         core_copies[h] = copy
         sends.append(copy)
 
+    def edges_of(h, t, xs):
+        i_low = (xs + NX - seam_low) % NX + t * NX
+        i_up = (xs + seam_up) % NX + t * NX
+        return jnp.concatenate([edge[h, 0, i_low], edge[h, 1, i_up]], axis=0), i_low, i_up
+
     def mains(h):
+        dq = dot_tn(dst[:last_row], kv[h, 0:NX].reshape(last_row, HS))
+        dq += dot_tn(dst[last_row:tab_row], gsel[h, 0].reshape(2 * BLK, HS))
+        for xs in range(NX):
+            part = slice(xs * 2 * BLK, (xs + 1) * 2 * BLK)
+            k_edge = edges_of(h, 0, xs)[0]
+            dq_edge = dot_tn(dst[tab_row:, part], k_edge)
+            dqs[h, xs] = (dq[part] + dq_edge).astype(BF16).reshape(2, BLK, HS)
+            for t, lists in ((0, dst), (1, pt)):
+                rows = qd[h, t * NX + xs].reshape(2 * BLK, HS)
+                grad = dot_nn(lists[tab_row:, part], rows).astype(BF16)
+                _, i_low, i_up = edges_of(h, t, xs)
+                edge_s[h, 0, i_low] = grad[:BLK]
+                edge_s[h, 1, i_up] = grad[BLK:]
         for t, lists in ((0, dst), (1, pt)):
             rows = qd[h, t * NX : (t + 1) * NX].reshape(NX * 2 * BLK, HS)
             grad = dot_nn(lists[:last_row], rows)
@@ -478,7 +495,8 @@
             )
 
     last = hx - 1
-    send_edges(0)
+    for h in range(hx):
+        send_edges(h)
     hear_word(1)
     for h in range(hx):
         for way in range(2):
@@ -490,10 +508,9 @@
             hear_word(3)
             send_ids()
         tables(h)
-        send_back(h)
         if h < last:
             mains(h)
-            send_edges(h + 1)
+            send_back(h)
             hear_word(4)
             y_start(h)
     hear_word(5)
@@ -501,13 +518,15 @@
         copy.wait_recv()
     for h in range(last):
         z_start(h)
+    y_start(last)
     mains(last)
-    y_start(last)
+    send_back(last)
     for h in range(hx):
         send_dq(h)
-    for h in range(hx):
+    for h in range(last):
         finish(h)
     z_start(last)
+    finish(last)
     for h in range(hx):
         z_end(h)
 
@@ -590,33 +609,24 @@
         copy.wait()
 
 
-def last_step(dq_in, dk_in, dv_in, dg_in, dq_out, dk_out, dv_out, dg_out, rows, narrow, full, got, put):
-    parts = narrow.shape[0]
-    loads = []
-    for i in range(parts):
-        loads.append(
-            pltpu.make_async_copy(dg_in.at[i // NX, i % NX], narrow.at[i], got.at[i])
-        )
-    for i, src in enumerate((dq_in, dk_in, dv_in)):
-        loads.append(pltpu.make_async_copy(src.at[0], rows.at[i], got.at[parts + i]))
-    for copy in loads:
-        copy.start()
+def last_step(dq_in, dk_in, dv_in, dg_in, dq_out, dk_out, dv_out, dg_out, full, put):
+    kinds, parts, _, heads = dg_in.shape[:4]
     stores = []
-    for i in range(parts):
-        loads[i].wait()
-        for h in range(narrow.shape[2]):
-            for b in range(TABLE):
-                rows_b = narrow[i, :, h, b].astype(F32).reshape(BLK, HS)
-                full[i, b, :, h * HS : (h + 1) * HS] = rows_b
-        cols = pl.ds(i % NX * full.shape[3], full.shape[3])
-        copy = pltpu.make_async_copy(full.at[i], dg_out.at[i // NX, :, :, cols], put.at[i])
-        copy.start()
-        stores.append(copy)
-    for i, dst_ref in enumerate((dq_out, dk_out, dv_out)):
-        loads[parts + i].wait()
-        copy = pltpu.make_async_copy(rows.at[i], dst_ref.at[0], put.at[parts + i])
-        copy.start()
-        stores.append(copy)
+    for kind in range(kinds):
+        for xs in range(parts):
+            i = kind * parts + xs
+            for h in range(heads):
+                for b in range(TABLE):
+                    rows_b = dg_in[kind, xs, :, h, b].astype(F32).reshape(BLK, HS)
+                    full[i, b, :, h * HS : (h + 1) * HS] = rows_b
+            cols = pl.ds(xs * full.shape[3], full.shape[3])
+            stores.append(
+                pltpu.make_async_copy(full.at[i], dg_out.at[kind, :, :, cols], put.at[i])
+            )
+            stores[-1].start()
+    for i, (src, dst_ref) in enumerate(((dq_in, dq_out), (dk_in, dk_out), (dv_in, dv_out))):
+        stores.append(pltpu.make_async_copy(src, dst_ref, put.at[kinds * parts + i]))
+        stores[-1].start()
     for copy in stores:
         copy.wait()
 
@@ -629,19 +639,19 @@
     rows_y = BLK // ny
     blocks = [a.reshape(2, BLK, hd) for a in (query, key, value, dout)]
     rand = jnp.transpose(rand_blocks, (2, 0, 1))
+    operands = (glob_ids, rand, *blocks, glob_keys, glob_values)
     vm = pltpu.VMEM
     dma = pltpu.SemaphoreType.DMA
     out = jax.ShapeDtypeStruct((2, BLK, hd), BF16)
     anywhere = pl.BlockSpec(memory_space=pltpu.HBM)
-    scalars = pl.BlockSpec(memory_space=pltpu.SMEM)
     scratch = [
         vm((hx, 2 * NX, 2, BLK, HS), BF16),
         vm((hx, 2 * NX, 2, BLK, HS), BF16),
         vm((hx, 2, 2 * NX, BLK, HS), BF16),
         vm((2, TABLE, BLK, wide), BF16),
         vm((hx, 2, 2, BLK, HS), BF16),
-        vm((10 * BLK, NX * 2 * BLK), BF16),
-        vm((10 * BLK, NX * 2 * BLK), BF16),
+        vm((12 * BLK, NX * 2 * BLK), BF16),
+        vm((12 * BLK, NX * 2 * BLK), BF16),
         vm((hx, NX, 2, BLK, HS), BF16),
         vm((hx, 2 * NX, 2, BLK, HS), F32),
         vm((hx, 2 * NX, 2, BLK, HS), BF16),
@@ -687,17 +697,20 @@
         dma((4, ny)),
         dma((4, ny)),
         pltpu.SemaphoreType.REGULAR((max(ny, nz) // 2, 4)),
+        pltpu.SMEM(glob_ids.shape, jnp.int32),
+        pltpu.SMEM(rand.shape, jnp.int32),
+        dma((2,)),
     ]
     dq, dk, dv, dg = pl.pallas_call(
         functools.partial(body, nz, ny, hx),
         out_shape=(out, out, out, jax.ShapeDtypeStruct((2, NX, ny, hx, TABLE, rows_y, HS), BF16)),
-        in_specs=[scalars, scalars] + [anywhere] * 6,
+        in_specs=[pl.BlockSpec(memory_space=pltpu.HBM)] * 8,
         out_specs=(anywhere,) * 4,
         scratch_shapes=scratch,
         compiler_params=pltpu.CompilerParams(
-            collective_id=0, has_side_effects=True, vmem_limit_bytes=60 * 1024 * 1024
+            collective_id=0, has_side_effects=True, vmem_limit_bytes=40 * 1024 * 1024
         ),
-    )(glob_ids, rand, *blocks, glob_keys, glob_values)
+    )(*[pltpu.with_memory_space_constraint(a, pltpu.HBM) for a in operands])
     rows = jax.ShapeDtypeStruct((1, 2 * BLK, hd), BF16)
     dq, dk, dv = (a.reshape(1, 2 * BLK, hd) for a in (dq, dk, dv))
     parts = 2 * NX
@@ -705,16 +718,13 @@
         pl.pallas_call(
             last_step,
             out_shape=(rows, rows, rows, jax.ShapeDtypeStruct((2, TABLE, BLK, hd), F32)),
-            in_specs=[anywhere] * 4,
+            in_specs=[pl.BlockSpec(memory_space=pltpu.VMEM)] * 4,
             out_specs=(anywhere,) * 4,
             scratch_shapes=[
-                vm((3, 2 * BLK, hd), BF16),
-                vm((parts, ny, hx, TABLE, rows_y, HS), BF16),
                 vm((parts, TABLE, BLK, wide), F32),
                 dma((parts + 3,)),
-                dma((parts + 3,)),
             ],
-            compiler_params=pltpu.CompilerParams(vmem_limit_bytes=60 * 1024 * 1024),
+            compiler_params=pltpu.CompilerParams(vmem_limit_bytes=16 * 1024 * 1024),
         )(dq, dk, dv, dg)
     )
 

time: 73.1 us -> 65.8 us (0.900)
  Pallas kernels: 72.2 us -> 65 us
    pallas_call x1, Pallas kernels: 69.5 us -> 63.3 us  [on_device(): pl.pallas_call(functools.partial(body, nz, ny, hx), out_shape=(out, out,...]
    pallas_call x1, Pallas kernels: 2.68 us -> 1.68 us  [on_device(): pl.pallas_call(last_step, out_shape=(rows, rows, rows, jax.ShapeDtypeStru...]
where the time goes in v4:
time: 65.8 us; the launch traced here: 65.6 us
  Pallas kernels  65 us (99%)
    pallas_call x1, Pallas kernels, on_device(): pl.pallas_call(functools.partial(body, nz, ny, hx), out_shape=(out, out,...  63.3 us
    pallas_call x1, Pallas kernels, on_device(): pl.pallas_call(last_step, out_shape=(rows, rows, rows, jax.ShapeDtypeStru...  1.68 us

profile of v4, /device:TPU:1, one launch (start us, length us, event | category | flops | bytes accessed | tf_op | source)
XLA Modules:
  0.0 65.6 jit_solution(12179841473405592767)
XLA Ops:
  0.6 63.3 %shard_map.111 = (bf16[2,64,1024]{2,1,0:T(8,128)(2,1)S(1)}, bf16[2,64,1024]{2,1,0:T(8,128)(2,1)S(1)}, bf16[2,64,1024]{2,1,0:T(8,128)(2,1)S(1)}, bf16[2,4,8,2,4,8,128]{6,5,4,3,2,1,0:T(8,128)(2,1)S(1)}) custom-call(s32[1,2]{1,0:T(1,128)} %ids_in.1, s32[3,8,192]{2,1,0:T(8,128)} %bitcast.15, bf16[2,64,1024]{2,1,0:T(8,128)(2,1)} %bitcast.11, ...), custom_call_target="tpu_custom_call" | custom-call | tf_op jit(solution)/shard_map/pallas_call | solution.py:704
  64.0 1.7 %shard_map.112 = (bf16[1,128,1024]{2,1,0:T(8,128)(2,1)}, bf16[1,128,1024]{2,1,0:T(8,128)(2,1)}, bf16[1,128,1024]{2,1,0:T(8,128)(2,1)}, f32[2,4,64,1024]{3,2,1,0:T(8,128)}) custom-call(bf16[1,128,1024]{2,1,0:T(8,128)(2,1)S(1)} %bitcast.8, bf16[1,128,1024]{2,1,0:T(8,128)(2,1)S(1)} %bitcast.9, bf16[1,128,1024]{2,1,0:T(8,128)(2,1)S(1)} %bitcast.10, ...), custom_call_target="tpu_custom_call" | custom-call | tf_op jit(solution)/shard_map/pallas_call | solution.py:718

commit v5 on v4

--- a/solution.py
+++ b/solution.py
@@ -70,7 +70,6 @@
     y_recv,
     z_all,
     y_all,
-    table,
     in_loc,
     in_snd,
     in_rcv,
@@ -96,7 +95,6 @@
     yg_snd,
     yg_rcv,
     xg_loc,
-    t_out,
     xg_snd,
     xg_rcv,
     cg_snd,
@@ -531,7 +529,7 @@
         z_end(h)
 
     def table_out(kind, yy, xs):
-        return table.at[kind, xs, yy]
+        return dg_out.at[kind, xs, yy]
 
     for j in outward(ny)[::-1]:
         to = (y + j) % ny
@@ -579,34 +577,21 @@
             ).wait_recv()
             to_sibling(table_out(c, yy, frm), yy, frm, j, d)
 
+    near = outward(ny)[::-1]
     spread(0)
-    before = [0]
-    near = outward(ny)[::-1]
-    for start in range(0, len(near), 2):
-        group = near[start : start + 2]
-        for d in group:
-            frm = (y + ny - d) % ny
-            remote(
-                y_all.at[frm], y_all.at[frm], yg_snd.at[d - 1], yg_rcv.at[d - 1], ctx, frm
-            ).wait_recv()
-            spread(d)
-        for d in before:
-            pass_on(d)
-        before = group
-    for d in before:
+    for d in near:
+        frm = (y + ny - d) % ny
+        remote(y_all.at[frm], y_all.at[frm], yg_snd.at[d - 1], yg_rcv.at[d - 1], ctx, frm).wait_recv()
+        spread(d)
+    for d in [0] + near:
         pass_on(d)
 
     for copy in locals_out:
         copy.wait()
-    final = [pltpu.make_async_copy(table.at[k], dg_out.at[k], t_out.at[i]) for i, k in enumerate((c, 1 - c))]
-    final[0].start()
     for copy in pending:
         copy.wait_recv()
-    final[1].start()
     for copy in sends:
         copy.wait_send()
-    for copy in final:
-        copy.wait()
 
 
 def last_step(dq_in, dk_in, dv_in, dg_in, dq_out, dk_out, dv_out, dg_out, full, put):
@@ -665,7 +650,6 @@
         vm((hx, ny, 2, rows_y, HS), BF16),
         vm((hx, nz, TABLE, rows_y, HS), BF16),
         vm((ny, hx, TABLE, rows_y, HS), BF16),
-        vm((2, NX, ny, hx, TABLE, rows_y, HS), BF16),
         dma((hx, 4)),
         dma((hx, 4, 3)),
         dma((hx, 4, 3)),
@@ -691,7 +675,6 @@
         dma((ny,)),
         dma((ny,)),
         dma((ny,)),
-        dma((2,)),
         dma((3, ny)),
         dma((3, ny)),
         dma((4, ny)),

time: 65.8 us -> 63 us (0.957)
  Pallas kernels: 65 us -> 62.3 us
    pallas_call x1, Pallas kernels: 63.3 us -> 60.6 us  [on_device(): pl.pallas_call(functools.partial(body, nz, ny, hx), out_shape=(out, out,...]
where the time goes in v5:
time: 63 us; the launch traced here: 62.9 us
  Pallas kernels  62.3 us (99%)
  between operations  0.64 us (1%)
    pallas_call x1, Pallas kernels, on_device(): pl.pallas_call(functools.partial(body, nz, ny, hx), out_shape=(out, out,...  60.6 us
    pallas_call x1, Pallas kernels, on_device(): pl.pallas_call(last_step, out_shape=(rows, rows, rows, jax.ShapeDtypeStru...  1.68 us

profile of v5, /device:TPU:1, one launch (start us, length us, event | category | flops | bytes accessed | tf_op | source)
XLA Modules:
  0.0 62.9 jit_solution(16953604432499250218)
XLA Ops:
  0.6 60.6 %shard_map.111 = (bf16[2,64,1024]{2,1,0:T(8,128)(2,1)S(1)}, bf16[2,64,1024]{2,1,0:T(8,128)(2,1)S(1)}, bf16[2,64,1024]{2,1,0:T(8,128)(2,1)S(1)}, bf16[2,4,8,2,4,8,128]{6,5,4,3,2,1,0:T(8,128)(2,1)S(1)}) custom-call(s32[1,2]{1,0:T(1,128)} %ids_in.1, s32[3,8,192]{2,1,0:T(8,128)} %bitcast.15, bf16[2,64,1024]{2,1,0:T(8,128)(2,1)} %bitcast.11, ...), custom_call_target="tpu_custom_call" | custom-call | tf_op jit(solution)/shard_map/pallas_call | solution.py:687
  61.2 1.7 %shard_map.112 = (bf16[1,128,1024]{2,1,0:T(8,128)(2,1)}, bf16[1,128,1024]{2,1,0:T(8,128)(2,1)}, bf16[1,128,1024]{2,1,0:T(8,128)(2,1)}, f32[2,4,64,1024]{3,2,1,0:T(8,128)}) custom-call(bf16[1,128,1024]{2,1,0:T(8,128)(2,1)S(1)} %bitcast.8, bf16[1,128,1024]{2,1,0:T(8,128)(2,1)S(1)} %bitcast.9, bf16[1,128,1024]{2,1,0:T(8,128)(2,1)S(1)} %bitcast.10, ...), custom_call_target="tpu_custom_call" | custom-call | tf_op jit(solution)/shard_map/pallas_call | solution.py:701
